TPU v7x, 512 devices: a whole 4x8x8 slice. The times are simulated.
512 devices in a mesh: rows: 64 (over y, z), cols: 8 (over x, core).
Axes of the slice: x: 4, y: 8, z: 8, core: 2. Of those that a mesh axis runs over, the one named last changes fastest.
Arguments:
- patches: bfloat16 [512, 512, 512], P('rows', 'cols'), may hold values from -6 to 6
- tissue: int32 [512, 512], P('rows', 'cols'), may hold values 0 or 1
- w_value: bfloat16 [512, 512], replicated, may hold values from -0.25 to 0.25
- w_across: bfloat16 [512, 40], replicated, may hold values from -0.25 to 0.25
- w_down: bfloat16 [512, 40], replicated, may hold values from -0.25 to 0.25
- w_gate: bfloat16 [512, 512], replicated, may hold values from -0.25 to 0.25
- w_out: bfloat16 [512, 512], replicated, may hold values from -0.25 to 0.25
- step_bias_across: float32 [8], replicated, may hold values from -4.5 to -2.5
- step_bias_down: float32 [8], replicated, may hold values from -4.5 to -2.5
- rates_across: float32 [8], replicated, may hold values from 0.00390625 to 1
- rates_down: float32 [8], replicated, may hold values from 0.00390625 to 1
- skip_across: float32 [8], replicated, may hold values from 0.5 to 1.5
- skip_down: float32 [8], replicated, may hold values from 0.5 to 1.5
- gain_across: float32 [512], replicated, may hold values from 0.5 to 1.5
- gain_final: float32 [512], replicated, may hold values from 0.5 to 1.5
Outputs:
- mixed: bfloat16 [512, 512, 512], P('rows', 'cols')
Inputs may be any that keep to these rules, and one draw needn't show every extreme that they name: 1 marks a tissue patch, 0 background.
All inputs are finite; a program needn't handle non-finite values. No bound on the sum of `tissue` on one device may be relied on, other than what follows from the above.
Results may differ from a plain program's by a relative error of at most 0.015.
Values may be sent and summed in bfloat16 or wider, within the bound.
No kernel may reach another device: no remote copies, remote signals or barrier semaphores. Data moves between devices by JAX's collectives and lax.ppermute only.
A program may use at most 64 MiB of HBM per device.

v0:
```python
import math

import jax
import jax.numpy as jnp
from jax import lax
from jax.sharding import PartitionSpec as P

highest = lax.Precision.HIGHEST


def shifted(value, axis, by):
    count = lax.axis_size(axis)
    pairs = [(i, i + by) for i in range(count) if 0 <= i + by < count]
    return lax.ppermute(value, axis, pairs)


def scan_parts(values, b_rows, c_rows, step_sizes, rates, skips):
    line_count, length, head_count, head_width = values.shape
    state_count = b_rows.shape[-1]
    block_len = math.gcd(length, 128)
    block_count = length // block_len
    narrow = values.reshape(line_count, block_count, block_len, head_count, head_width)
    b_blocks = b_rows.reshape(line_count, block_count, block_len, state_count)
    c_blocks = c_rows.reshape(line_count, block_count, block_len, state_count)
    step_blocks = step_sizes.reshape(line_count, block_count, block_len, head_count)
    running = jnp.cumsum(-step_blocks * rates, axis=2)
    causal = (jnp.arange(block_len)[:, None] >= jnp.arange(block_len)[None, :])[
        None, None, :, :, None
    ]
    spans = jnp.where(causal, running[:, :, :, None, :] - running[:, :, None, :, :], 0.0)
    decays = jnp.where(causal, jnp.exp(spans), 0.0)
    intersections = jnp.einsum("lctn,lcsn->lcts", c_blocks, b_blocks, precision=highest)
    weights = (decays * intersections[..., None] * step_blocks[:, :, None, :, :]).astype(
        jnp.bfloat16
    )
    within = jnp.einsum("lctsh,lcshp->lcthp", weights, narrow, preferred_element_type=jnp.float32)
    to_end = jnp.exp(running[:, :, -1:, :] - running) * step_blocks
    push_coef = (b_blocks[..., :, None] * to_end[..., None, :]).astype(jnp.bfloat16)
    pushed = jnp.einsum("lcsnh,lcshp->lchnp", push_coef, narrow, preferred_element_type=jnp.float32)
    totals = running[:, :, -1, :]

    def advance(entered, item):
        pushed_one, total_one = item
        return (jnp.exp(total_one)[..., None, None] * entered + pushed_one, entered)

    final, entering = lax.scan(
        advance,
        jnp.zeros_like(pushed[:, 0]),
        (jnp.moveaxis(pushed, 1, 0), jnp.moveaxis(totals, 1, 0)),
    )
    entering = jnp.moveaxis(entering, 0, 1)
    carried = (
        jnp.einsum("lctn,lchnp->lcthp", c_blocks, entering, precision=highest)
        * jnp.exp(running)[..., None]
    )
    outputs = within + carried + skips[:, None] * narrow.astype(jnp.float32)
    before = jnp.cumsum(totals, axis=1) - totals
    reach = jnp.exp(before[:, :, None, :] + running)
    return (
        outputs.reshape(line_count, length, head_count * head_width),
        final,
        jnp.sum(totals, axis=1),
        reach.reshape(line_count, length, head_count),
    )


def line_scan(values, projected, step_bias, rates, skips):
    head_count = rates.shape[0]
    state_count = (projected.shape[-1] - head_count) // 2
    line_count, length, width_all = values.shape
    b_rows = projected[..., :state_count]
    c_rows = projected[..., state_count : 2 * state_count]
    step_sizes = jax.nn.softplus(projected[..., 2 * state_count :] + step_bias)
    parts = scan_parts(
        values.reshape(line_count, length, head_count, width_all // head_count),
        b_rows,
        c_rows,
        step_sizes,
        rates,
        skips,
    )
    return parts + (c_rows,)


def add_start(outputs, c_rows, reach, start):
    line_count, length, width_all = outputs.shape
    extra = jnp.einsum("ltn,lhnp->lthp", c_rows, start, precision=highest) * reach[..., None]
    return outputs + extra.reshape(line_count, length, width_all)


def rms_norm(values, gain):
    return values * lax.rsqrt(jnp.mean(values * values, axis=-1, keepdims=True) + 1e-05) * gain


def on_device(
    patches,
    tissue,
    w_value,
    w_across,
    w_down,
    w_gate,
    w_out,
    step_bias_across,
    step_bias_down,
    rates_across,
    rates_down,
    skip_across,
    skip_down,
    gain_across,
    gain_final,
):
    masked = patches * tissue.astype(jnp.bfloat16)[..., None]
    values_across = jnp.dot(masked, w_value, preferred_element_type=jnp.float32).astype(
        jnp.bfloat16
    )
    proj_across = jnp.dot(masked, w_across, preferred_element_type=jnp.float32)
    y_across, final, total, reach, c_rows = line_scan(
        values_across, proj_across, step_bias_across, rates_across, skip_across
    )
    decay_all = jnp.exp(total)[..., None, None]

    def relay(turn_index, entered):
        return shifted((decay_all * entered + final).astype(jnp.bfloat16), "cols", 1).astype(
            jnp.float32
        )

    start = lax.fori_loop(0, lax.axis_size("cols") - 1, relay, jnp.zeros_like(final))
    line_out = rms_norm(add_start(y_across, c_rows, reach, start), gain_across).astype(jnp.bfloat16)
    band_shape = line_out.shape
    split_count = lax.axis_size("rows")
    banded = line_out.reshape(
        band_shape[0], split_count, band_shape[1] // split_count, band_shape[2]
    )
    columns = jnp.moveaxis(
        lax.all_to_all(banded, "rows", split_axis=1, concat_axis=0, tiled=True)[:, 0], 1, 0
    )
    proj_down = jnp.dot(columns, w_down, preferred_element_type=jnp.float32)
    y_down = line_scan(columns, proj_down, step_bias_down, rates_down, skip_down)[0]
    column_vals = jnp.moveaxis(y_down.astype(jnp.bfloat16), 0, 1)[:, None]
    column_out = lax.all_to_all(
        column_vals, "rows", split_axis=0, concat_axis=1, tiled=True
    ).reshape(band_shape)
    gate = jnp.dot(masked, w_gate, preferred_element_type=jnp.float32)
    act = (rms_norm(column_out.astype(jnp.float32), gain_final) * jax.nn.silu(gate)).astype(
        jnp.bfloat16
    )
    return (
        masked.astype(jnp.float32) + jnp.dot(act, w_out, preferred_element_type=jnp.float32)
    ).astype(jnp.bfloat16)


def solution(mesh):
    return jax.shard_map(
        on_device,
        mesh=mesh,
        in_specs=(
            P("rows", "cols", None),
            P("rows", "cols"),
            P(),
            P(),
            P(),
            P(),
            P(),
            P(),
            P(),
            P(),
            P(),
            P(),
            P(),
            P(),
            P(),
        ),
        out_specs=P("rows", "cols", None),
        check_vma=False,
    )
```

profile of v0, /device:TPU:18, one launch (start us, length us, event | category | flops | bytes accessed | tf_op | source)
XLA Modules:
  0.0 170.1 jit_solution(15267115370229202984)
XLA Ops:
  3.2 6.3 %fusion.75 = f32[8,1,64,8]{3,0,1,2:T(8,128)S(1)} fusion(f32[8,1,64,8]{3,0,1,2:T(8,128)S(1)} %copy.84), kind=kOutput, calls=%fused_computation.115 | output fusion | flops 258048 | bytes 32768 | tf_op jit(solution)/shard_map/jit(cumsum)/reduce_window_sum | solution.py:26
  12.5 3.1 %fusion.47 = f32[8,64,8,64]{1,3,2,0:T(8,128)} fusion(f32[8,64,40]{1,2,0:T(8,128)S(1)} %fusion.39), kind=kOutput, calls=%fused_computation.67 | convolution fusion | flops 50331648 | bytes 1114112 | tf_op jit(solution)/shard_map/lctn,lchnp->lcthp/dot_general | solution.py:53
  16.7 55.3 %while.29 = (s32[]{:T(128)}, f32[8,8,16,64]{3,2,1,0:T(8,128)S(1)}, f32[8,8,1,1]{1,0,3,2:T(8,128)S(1)}, f32[8,8,16,64]{3,2,1,0:T(8,128)S(1)}, s32[]{:T(128)}, /*index=5*/s32[]{:T(128)}) while((s32[]{:T(128)}, f32[8,8,16,64]{3,2,1,0:T(8,128)S(1)}, f32[8,8,1,1]{1,0,3,2:T(8,128)S(1)}, f32[8,8,16,64]{3,2,1,0:T(8,128)S(1)}, s32[]{:T(128)}, ...), condition=%wide.region_2.3_spmd.clone, body=%wide.region_1.2_spmd.clone.sunk | while | flops 327683 | bytes 1573239 | solution.py:127
  16.8 1.9 %collective-permute-start = (bf16[8,8,16,64]{3,2,1,0:T(8,128)(2,1)S(1)}, bf16[8,8,16,64]{3,2,1,0:T(8,128)(2,1)S(1)}, u32[]{:S(2)}, u32[]{:S(2)}) collective-permute-start(bf16[8,8,16,64]{3,2,1,0:T(8,128)(2,1)S(1)} %fusion.83), channel_id=1, source_target_pairs={{0,1},{1,2},{2,3},{3,4},{4,5},{5,6},{6,7},{8,9},{9,10},{10,11},{11... | collective-permute-start | bytes 393224 | tf_op jit(solution)/shard_map/while/body/eval_jaxpr/ppermute | solution.py:14
  18.8 5.8 %collective-permute-done = bf16[8,8,16,64]{3,2,1,0:T(8,128)(2,1)S(1)} collective-permute-done((bf16[8,8,16,64]{3,2,1,0:T(8,128)(2,1)S(1)}, bf16[8,8,16,64]{3,2,1,0:T(8,128)(2,1)S(1)}, u32[]{:S(2)}, u32[]{:S(2)}) %collective-permute-start) | collective-permute-done | bytes 131104 | tf_op jit(solution)/shard_map/while/body/eval_jaxpr/ppermute | solution.py:14
  24.7 1.9 %collective-permute-start = (bf16[8,8,16,64]{3,2,1,0:T(8,128)(2,1)S(1)}, bf16[8,8,16,64]{3,2,1,0:T(8,128)(2,1)S(1)}, u32[]{:S(2)}, u32[]{:S(2)}) collective-permute-start(bf16[8,8,16,64]{3,2,1,0:T(8,128)(2,1)S(1)} %fusion.83), channel_id=1, source_target_pairs={{0,1},{1,2},{2,3},{3,4},{4,5},{5,6},{6,7},{8,9},{9,10},{10,11},{11... | collective-permute-start | bytes 393224 | tf_op jit(solution)/shard_map/while/body/eval_jaxpr/ppermute | solution.py:14
  26.6 5.8 %collective-permute-done = bf16[8,8,16,64]{3,2,1,0:T(8,128)(2,1)S(1)} collective-permute-done((bf16[8,8,16,64]{3,2,1,0:T(8,128)(2,1)S(1)}, bf16[8,8,16,64]{3,2,1,0:T(8,128)(2,1)S(1)}, u32[]{:S(2)}, u32[]{:S(2)}) %collective-permute-start) | collective-permute-done | bytes 131104 | tf_op jit(solution)/shard_map/while/body/eval_jaxpr/ppermute | solution.py:14
  32.6 1.9 %collective-permute-start = (bf16[8,8,16,64]{3,2,1,0:T(8,128)(2,1)S(1)}, bf16[8,8,16,64]{3,2,1,0:T(8,128)(2,1)S(1)}, u32[]{:S(2)}, u32[]{:S(2)}) collective-permute-start(bf16[8,8,16,64]{3,2,1,0:T(8,128)(2,1)S(1)} %fusion.83), channel_id=1, source_target_pairs={{0,1},{1,2},{2,3},{3,4},{4,5},{5,6},{6,7},{8,9},{9,10},{10,11},{11... | collective-permute-start | bytes 393224 | tf_op jit(solution)/shard_map/while/body/eval_jaxpr/ppermute | solution.py:14
  34.5 5.8 %collective-permute-done = bf16[8,8,16,64]{3,2,1,0:T(8,128)(2,1)S(1)} collective-permute-done((bf16[8,8,16,64]{3,2,1,0:T(8,128)(2,1)S(1)}, bf16[8,8,16,64]{3,2,1,0:T(8,128)(2,1)S(1)}, u32[]{:S(2)}, u32[]{:S(2)}) %collective-permute-start) | collective-permute-done | bytes 131104 | tf_op jit(solution)/shard_map/while/body/eval_jaxpr/ppermute | solution.py:14
  40.5 1.9 %collective-permute-start = (bf16[8,8,16,64]{3,2,1,0:T(8,128)(2,1)S(1)}, bf16[8,8,16,64]{3,2,1,0:T(8,128)(2,1)S(1)}, u32[]{:S(2)}, u32[]{:S(2)}) collective-permute-start(bf16[8,8,16,64]{3,2,1,0:T(8,128)(2,1)S(1)} %fusion.83), channel_id=1, source_target_pairs={{0,1},{1,2},{2,3},{3,4},{4,5},{5,6},{6,7},{8,9},{9,10},{10,11},{11... | collective-permute-start | bytes 393224 | tf_op jit(solution)/shard_map/while/body/eval_jaxpr/ppermute | solution.py:14
  42.4 5.8 %collective-permute-done = bf16[8,8,16,64]{3,2,1,0:T(8,128)(2,1)S(1)} collective-permute-done((bf16[8,8,16,64]{3,2,1,0:T(8,128)(2,1)S(1)}, bf16[8,8,16,64]{3,2,1,0:T(8,128)(2,1)S(1)}, u32[]{:S(2)}, u32[]{:S(2)}) %collective-permute-start) | collective-permute-done | bytes 131104 | tf_op jit(solution)/shard_map/while/body/eval_jaxpr/ppermute | solution.py:14
  50.3 5.8 %collective-permute-done = bf16[8,8,16,64]{3,2,1,0:T(8,128)(2,1)S(1)} collective-permute-done((bf16[8,8,16,64]{3,2,1,0:T(8,128)(2,1)S(1)}, bf16[8,8,16,64]{3,2,1,0:T(8,128)(2,1)S(1)}, u32[]{:S(2)}, u32[]{:S(2)}) %collective-permute-start) | collective-permute-done | bytes 131104 | tf_op jit(solution)/shard_map/while/body/eval_jaxpr/ppermute | solution.py:14
  58.2 5.8 %collective-permute-done = bf16[8,8,16,64]{3,2,1,0:T(8,128)(2,1)S(1)} collective-permute-done((bf16[8,8,16,64]{3,2,1,0:T(8,128)(2,1)S(1)}, bf16[8,8,16,64]{3,2,1,0:T(8,128)(2,1)S(1)}, u32[]{:S(2)}, u32[]{:S(2)}) %collective-permute-start) | collective-permute-done | bytes 131104 | tf_op jit(solution)/shard_map/while/body/eval_jaxpr/ppermute | solution.py:14
  66.1 5.8 %collective-permute-done = bf16[8,8,16,64]{3,2,1,0:T(8,128)(2,1)S(1)} collective-permute-done((bf16[8,8,16,64]{3,2,1,0:T(8,128)(2,1)S(1)}, bf16[8,8,16,64]{3,2,1,0:T(8,128)(2,1)S(1)}, u32[]{:S(2)}, u32[]{:S(2)}) %collective-permute-start) | collective-permute-done | bytes 131104 | tf_op jit(solution)/shard_map/while/body/eval_jaxpr/ppermute | solution.py:14
  72.0 4.4 %convolution_multiply_fusion = f32[8,64,8,64]{1,3,2,0:T(8,128)S(1)} fusion(f32[8,8,16,64]{3,2,1,0:T(8,128)S(1)} %get-tuple-element.69, f32[8,64,8]{1,2,0:T(8,128)S(1)} %get-tuple-element.153, f32[8,64,40]{1,2,0:T(8,128)} %copy-done.4), kind=kOutput, calls=%fused_computation.15 | convolution fusion | flops 50593792 | bytes 1392640 | tf_op jit(solution)/shard_map/ltn,lhnp->lthp/dot_general | solution.py:87
  76.4 4.6 %fusion.6 = (f32[8,64]{1,0:T(8,128)S(1)}, f32[8,1,64,8,64]{2,4,3,0,1:T(8,128)}) fusion(f32[8,64,8,64]{1,3,2,0:T(8,128)S(1)} %convolution_multiply_fusion, f32[8,1,64,8,64]{2,4,3,0,1:T(8,128)S(1)} %bitcast.151, f32[8]{0:T(128)S(1)} %copy-done.8, f32[8,64,8,64]{1,3,2,0:T(8,128)} %fusion.47, f32[8,64,8]{1,2,0:T(8,128)S(1)} %get-tuple-element.154, ...), kind=kOutput, calls=%fused_computation.12 | convolution fusion | flops 36961792 | bytes 4904992 | tf_op jit(solution)/shard_map/lctsh,lcshp->lcthp/dot_general | solution.py:36
  81.0 3.5 %copy.89 = f32[8,64,1,512]{3,0,2,1:T(8,128)} copy(f32[8,64,1,512]{1,3,0,2:T(8,128)} %bitcast.152) | data formatting | bytes 2097152 | tf_op jit(solution)/shard_map/reshape | solution.py:60
  86.5 2.5 %multiply_convert_fusion.4 = bf16[8,64,1,512]{3,0,2,1:T(8,128)(2,1)} fusion(f32[8,64,1,512]{3,0,2,1:T(8,128)} %copy.89, f32[8,64,1,512]{3,0,2,1:T(8,128)} %copy.90, f32[512]{0:T(512)S(1)} %copy-done.6, f32[8,64]{0,1:T(8,128)S(1)} %copy.91), kind=kLoop, calls=%fused_computation.39 | loop fusion | flops 1048576 | bytes 2625536 | tf_op jit(solution)/shard_map/convert_element_type | solution.py:128
  89.0 16.5 %all-to-all-start = ((bf16[8,64,1,512]{3,0,2,1:T(8,128)(2,1)}), bf16[8,64,1,512]{3,0,2,1:T(8,128)(2,1)S(1)}, u32[]{:S(2)}, u32[]{:S(2)}) async-start(bf16[8,64,1,512]{3,0,2,1:T(8,128)(2,1)} %multiply_convert_fusion.4), calls=%async_computation | async-start | bytes 1048576 | tf_op jit(solution)/shard_map/all_to_all | solution.py:135
  105.5 18.6 %all-to-all-done = bf16[8,64,1,512]{3,0,2,1:T(8,128)(2,1)S(1)} async-done(((bf16[8,64,1,512]{3,0,2,1:T(8,128)(2,1)}), bf16[8,64,1,512]{3,0,2,1:T(8,128)(2,1)S(1)}, u32[]{:S(2)}, u32[]{:S(2)}) %all-to-all-start) | async-done | bytes 524320 | tf_op jit(solution)/shard_map/all_to_all | solution.py:135
  134.1 2.2 %fusion.10 = bf16[1,4,128,8,64]{2,4,3,1,0:T(8,128)(2,1)S(1)} fusion(f32[1,4,128,8,64]{2,4,3,1,0:T(8,128)S(1)} %fusion.7, bf16[4,128,8,64]{1,3,2,0:T(8,128)(2,1)S(1)} %copy.96, f32[1,4,128,8,64]{2,4,3,1,0:T(8,128)} %copy.102, f32[4,128,8]{1,2,0:T(8,128)S(1)} %get-tuple-element.143, f32[4,128,128]{2,1,0:T(8,128)S(1)} %fusion.63, ...), kind=kOutput, calls=%fused_computation.23 | convolution fusion | flops 71303168 | bytes 3457056 | tf_op jit(solution)/shard_map/lctsh,lcshp->lcthp/dot_general | solution.py:36
  138.0 3.8 %reduce.1 = bf16[512,512]{1,0:T(8,128)(2,1)S(1)} reduce(bf16[512,1,1,512]{3,2,1,0:T(2,128)(2,1)S(1)} %reshape.403, bf16[]{:T(256)} %broadcast.230), dimensions={1,2}, to_apply=%reshape.403.reduce_sub_computation | reduce | bytes 1048578 | tf_op jit(solution)/shard_map/convert_element_type | solution.py:139
  142.1 23.4 %all_to_all.24 = bf16[64,2,2048]{2,1,0:T(2,128)(2,1)S(1)} all-to-all(bf16[64,2,2048]{2,1,0:T(2,128)(2,1)S(1)} %reshape.404), channel_id=1, replica_groups=mesh['rows'=64,'cols'=8] {'rows'}, dimensions={0} | all-to-all | bytes 1048576 | tf_op jit(solution)/shard_map/all_to_all | solution.py:140
  166.7 3.4 %fusion.11 = bf16[8,64,512]{2,1,0:T(8,128)(2,1)} fusion(f32[64,8,1,1,512]{4,1,0,3,2:T(8,128)S(1)} %bitcast_convert_fusion, bf16[512,512]{1,0:T(8,128)(2,1)} %param.25, bf16[512,512]{1,0:T(8,128)(2,1)} %param.24, f32[512]{0:T(512)S(1)} %copy-done.12, f32[8,64]{1,0:T(8,128)S(1)} %add_rsqrt_fusion, bf16[8,64,512]{2,1,0:T(8,128)(2,1)S(1)} %copy-done.11, ...), kind=kOutput, calls=%fused_computation.24 | convolution fusion | flops 540803072 | bytes 3150848 | tf_op jit(solution)/shard_map/dot_general | solution.py:148
  (108 shorter events, 29.5 us)
Async XLA Ops:
  0.0 9.7 %copy-start = (bf16[512,512]{1,0:T(8,128)(2,1)S(1)}, bf16[512,512]{1,0:T(8,128)(2,1)}, u32[]{:S(2)}) copy-start(bf16[512,512]{1,0:T(8,128)(2,1)} %param.21) | copy-start | bytes 1572868
  0.0 9.8 %copy-start.10 = (bf16[8,64,512]{2,1,0:T(8,128)(2,1)S(1)}, bf16[8,64,512]{2,1,0:T(8,128)(2,1)}, u32[]{:S(2)}) copy-start(bf16[8,64,512]{2,1,0:T(8,128)(2,1)} %param.19) | copy-start | bytes 1572868
  2.3 13.3 %copy-start.4 = (f32[8,64,40]{1,2,0:T(8,128)}, f32[8,64,40]{1,2,0:T(8,128)S(1)}, u32[]{:S(2)}) copy-start(f32[8,64,40]{1,2,0:T(8,128)S(1)} %fusion.39) | copy-start | bytes 245764
  16.8 7.7 %collective-permute-start = (bf16[8,8,16,64]{3,2,1,0:T(8,128)(2,1)S(1)}, bf16[8,8,16,64]{3,2,1,0:T(8,128)(2,1)S(1)}, u32[]{:S(2)}, u32[]{:S(2)}) collective-permute-start(bf16[8,8,16,64]{3,2,1,0:T(8,128)(2,1)S(1)} %fusion.83), channel_id=1, source_target_pairs={{0,1},{1,2},{2,3},{3,4},{4,5},{5,6},{6,7},{8,9},{9,10},{10,11},{11... | collective-permute-start | bytes 393224 | tf_op jit(solution)/shard_map/while/body/eval_jaxpr/ppermute | solution.py:14
  24.7 7.7 %collective-permute-start = (bf16[8,8,16,64]{3,2,1,0:T(8,128)(2,1)S(1)}, bf16[8,8,16,64]{3,2,1,0:T(8,128)(2,1)S(1)}, u32[]{:S(2)}, u32[]{:S(2)}) collective-permute-start(bf16[8,8,16,64]{3,2,1,0:T(8,128)(2,1)S(1)} %fusion.83), channel_id=1, source_target_pairs={{0,1},{1,2},{2,3},{3,4},{4,5},{5,6},{6,7},{8,9},{9,10},{10,11},{11... | collective-permute-start | bytes 393224 | tf_op jit(solution)/shard_map/while/body/eval_jaxpr/ppermute | solution.py:14
  32.6 7.7 %collective-permute-start = (bf16[8,8,16,64]{3,2,1,0:T(8,128)(2,1)S(1)}, bf16[8,8,16,64]{3,2,1,0:T(8,128)(2,1)S(1)}, u32[]{:S(2)}, u32[]{:S(2)}) collective-permute-start(bf16[8,8,16,64]{3,2,1,0:T(8,128)(2,1)S(1)} %fusion.83), channel_id=1, source_target_pairs={{0,1},{1,2},{2,3},{3,4},{4,5},{5,6},{6,7},{8,9},{9,10},{10,11},{11... | collective-permute-start | bytes 393224 | tf_op jit(solution)/shard_map/while/body/eval_jaxpr/ppermute | solution.py:14
  40.5 7.7 %collective-permute-start = (bf16[8,8,16,64]{3,2,1,0:T(8,128)(2,1)S(1)}, bf16[8,8,16,64]{3,2,1,0:T(8,128)(2,1)S(1)}, u32[]{:S(2)}, u32[]{:S(2)}) collective-permute-start(bf16[8,8,16,64]{3,2,1,0:T(8,128)(2,1)S(1)} %fusion.83), channel_id=1, source_target_pairs={{0,1},{1,2},{2,3},{3,4},{4,5},{5,6},{6,7},{8,9},{9,10},{10,11},{11... | collective-permute-start | bytes 393224 | tf_op jit(solution)/shard_map/while/body/eval_jaxpr/ppermute | solution.py:14
  48.4 7.7 %collective-permute-start = (bf16[8,8,16,64]{3,2,1,0:T(8,128)(2,1)S(1)}, bf16[8,8,16,64]{3,2,1,0:T(8,128)(2,1)S(1)}, u32[]{:S(2)}, u32[]{:S(2)}) collective-permute-start(bf16[8,8,16,64]{3,2,1,0:T(8,128)(2,1)S(1)} %fusion.83), channel_id=1, source_target_pairs={{0,1},{1,2},{2,3},{3,4},{4,5},{5,6},{6,7},{8,9},{9,10},{10,11},{11... | collective-permute-start | bytes 393224 | tf_op jit(solution)/shard_map/while/body/eval_jaxpr/ppermute | solution.py:14
  56.3 7.7 %collective-permute-start = (bf16[8,8,16,64]{3,2,1,0:T(8,128)(2,1)S(1)}, bf16[8,8,16,64]{3,2,1,0:T(8,128)(2,1)S(1)}, u32[]{:S(2)}, u32[]{:S(2)}) collective-permute-start(bf16[8,8,16,64]{3,2,1,0:T(8,128)(2,1)S(1)} %fusion.83), channel_id=1, source_target_pairs={{0,1},{1,2},{2,3},{3,4},{4,5},{5,6},{6,7},{8,9},{9,10},{10,11},{11... | collective-permute-start | bytes 393224 | tf_op jit(solution)/shard_map/while/body/eval_jaxpr/ppermute | solution.py:14
  64.2 7.7 %collective-permute-start = (bf16[8,8,16,64]{3,2,1,0:T(8,128)(2,1)S(1)}, bf16[8,8,16,64]{3,2,1,0:T(8,128)(2,1)S(1)}, u32[]{:S(2)}, u32[]{:S(2)}) collective-permute-start(bf16[8,8,16,64]{3,2,1,0:T(8,128)(2,1)S(1)} %fusion.83), channel_id=1, source_target_pairs={{0,1},{1,2},{2,3},{3,4},{4,5},{5,6},{6,7},{8,9},{9,10},{10,11},{11... | collective-permute-start | bytes 393224 | tf_op jit(solution)/shard_map/while/body/eval_jaxpr/ppermute | solution.py:14
  71.9 4.5 %copy-start.3 = (f32[8,64,512]{1,2,0:T(8,128)S(1)}, f32[8,64,512]{1,2,0:T(8,128)}, u32[]{:S(2)}) copy-start(f32[8,64,512]{1,2,0:T(8,128)} %copy.109) | copy-start | bytes 3145732
  71.9 4.5 %copy-start.8 = (f32[8]{0:T(128)S(1)}, f32[8]{0:T(128)}, u32[]{:S(2)}) copy-start(f32[8]{0:T(128)} %param.30) | copy-start | bytes 100
  76.4 4.6 %copy-start.1 = (f32[8,64,8,64]{1,3,2,0:T(8,128)}, f32[8,64,8,64]{1,3,2,0:T(8,128)S(1)}, u32[]{:S(2)}) copy-start(f32[8,64,8,64]{1,3,2,0:T(8,128)S(1)} %convolution_multiply_fusion) | copy-start | bytes 3145732
  81.0 3.5 %copy-start.2 = (f32[8,64,8,64]{1,3,2,0:T(8,128)S(1)}, f32[8,64,8,64]{1,3,2,0:T(8,128)}, u32[]{:S(2)}) copy-start(f32[8,64,8,64]{1,3,2,0:T(8,128)} %copy-done.1) | copy-start | bytes 3145732
  84.5 1.9 %copy-start.6 = (f32[512]{0:T(512)S(1)}, f32[512]{0:T(512)}, u32[]{:S(2)}) copy-start(f32[512]{0:T(512)} %param.32) | copy-start | bytes 6148
  86.3 37.8 %copy-start.5 = (bf16[512,40]{0,1:T(8,128)(2,1)S(1)}, bf16[512,40]{0,1:T(8,128)(2,1)}, u32[]{:S(2)}) copy-start(bf16[512,40]{0,1:T(8,128)(2,1)} %param.23) | copy-start | bytes 122884
  86.4 38.0 %copy-start.7 = (f32[8]{0:T(128)S(1)}, f32[8]{0:T(128)}, u32[]{:S(2)}) copy-start(f32[8]{0:T(128)} %param.27) | copy-start | bytes 100
  86.5 38.2 %copy-start.9 = (f32[8]{0:T(128)S(1)}, f32[8]{0:T(128)}, u32[]{:S(2)}) copy-start(f32[8]{0:T(128)} %param.29) | copy-start | bytes 100
  89.0 35.2 %all-to-all-start = ((bf16[8,64,1,512]{3,0,2,1:T(8,128)(2,1)}), bf16[8,64,1,512]{3,0,2,1:T(8,128)(2,1)S(1)}, u32[]{:S(2)}, u32[]{:S(2)}) async-start(bf16[8,64,1,512]{3,0,2,1:T(8,128)(2,1)} %multiply_convert_fusion.4), calls=%async_computation | async-start | bytes 1048576 | tf_op jit(solution)/shard_map/all_to_all | solution.py:135
  130.0 4.0 %copy-start.13 = (f32[8]{0:T(128)S(1)}, f32[8]{0:T(128)}, u32[]{:S(2)}) copy-start(f32[8]{0:T(128)} %param.31) | copy-start | bytes 100
  165.5 1.3 copy-start.11
  165.5 1.3 copy-start.12
where the time goes:
time: 171 us; the launch traced here: 170 us
  waiting for transfers between devices  59 us (35%)
  starting transfers between devices  29.9 us (17%)
  matrix products  23.7 us (14%)
  blocking collectives  23.4 us (14%)
  other arithmetic  18.3 us (11%)
  local copies, waits for them, and re-layouts  15.1 us (9%)
    ppermute x7, waiting for transfers between devices, shifted(): return lax.ppermute(value, axis, pairs)  40.3 us
    all_to_all x1, blocking collectives, on_device(): lax.all_to_all(column_vals, 'rows', split_axis=0, concat_axis=1, tiled=True)  23.4 us
    all_to_all x1, waiting for transfers between devices, on_device(): lax.all_to_all(banded, 'rows', split_axis=1, concat_axis=0, tiled=True)  18.6 us
    all_to_all x1, starting transfers between devices, on_device(): lax.all_to_all(banded, 'rows', split_axis=1, concat_axis=0, tiled=True)  16.5 us
    ppermute x7, starting transfers between devices, shifted(): return lax.ppermute(value, axis, pairs)  13.4 us
    dot_general x2, matrix products, scan_parts(): jnp.einsum('lctsh,lcshp->lcthp', weights, narrow, preferred_element_type=...  6.8 us
    another operation x2, other arithmetic, scan_parts(): running = jnp.cumsum(-step_blocks * rates, axis=2)  6.59 us
    dot_general x2, matrix products, scan_parts(): jnp.einsum('lctn,lchnp->lcthp', c_blocks, entering, precision=highest)  4.91 us
  transfers between devices with their start and end apart: 8, of which 8 were waited for; matrix products, arithmetic and copies ran while one was open for 0% of the time, Pallas kernels for 0%

commit v1 on v0

v1 whole, which is shorter than its diff:
```python
import jax
import jax.numpy as jnp
from jax import lax
from jax.experimental import pallas as pl
from jax.experimental.pallas import tpu as pltpu
from jax.sharding import PartitionSpec as P

highest = lax.Precision.HIGHEST
bf16, f32 = jnp.bfloat16, jnp.float32
LANES = 128
CAP = 80.0


def iota(shape, dim):
    return lax.broadcasted_iota(jnp.int32, shape, dim)


def dot(a, b, precision=None):
    return jnp.dot(a, b, preferred_element_type=f32, precision=precision)


def halves(x):
    high = x.astype(bf16)
    return high, (x - high.astype(f32)).astype(bf16)


def softplus(v):
    return jnp.maximum(v, 0.0) + jnp.log1p(jnp.exp(-jnp.abs(v)))


def as_column(row):
    n = row.shape[-1]
    square = jnp.broadcast_to(row, (n, n))
    return jnp.sum(jnp.where(iota((n, n), 0) == iota((n, n), 1), square, 0.0), axis=1, keepdims=True)


def head_lanes(head_count, width):
    shape = (head_count, head_count * width)
    return jnp.where(iota(shape, 1) // width == iota(shape, 0), 1.0, 0.0)


def step_terms(proj_rows, bias, rates, group):
    head_count = bias.shape[-1]
    steps = softplus(proj_rows[-head_count:] + as_column(bias))
    falls = -steps * as_column(rates)
    logs = jnp.log(steps)
    blocks = proj_rows.shape[1] // LANES
    stack = lambda x: jnp.concatenate([x[:, k * LANES : (k + 1) * LANES] for k in range(blocks)], axis=0)
    falls, logs = stack(falls), stack(logs)
    source, target = iota((LANES, LANES), 0), iota((LANES, LANES), 1)
    same = source // group == target // group
    running = dot(falls, jnp.where(same & (source <= target), 1.0, 0.0), highest)
    totals = dot(falls, jnp.where(same, 1.0, 0.0), highest)
    return running, running - logs, totals


def products(proj_block, b_block):
    state_count = b_block.shape[0]
    rest = proj_block.shape[1] - 2 * state_count
    padded = jnp.concatenate(
        [jnp.zeros_like(b_block), b_block, jnp.zeros((rest, b_block.shape[1]), f32)], axis=0
    )
    return dot(proj_block, padded, highest)


def within(proj_block, b_block, group, run_col, less_row, values, block, head_count):
    source, target = iota((LANES, LANES), 1), iota((LANES, LANES), 0)
    keep = (source // group == target // group) & (source <= target)
    inter = jnp.where(keep, products(proj_block, b_block), 0.0)
    low_lanes = iota((LANES, LANES), 1) < LANES // 2
    tiles = []
    for pair in range(head_count // 2):
        weights = []
        for head in (2 * pair, 2 * pair + 1):
            at = block * head_count + head
            spans = run_col[:, at : at + 1] - less_row[at : at + 1, :]
            weights.append((jnp.exp(jnp.minimum(spans, CAP)) * inter).astype(bf16))
        both = dot(jnp.concatenate(weights, axis=0), values[:, pair * LANES : (pair + 1) * LANES])
        tiles.append(jnp.where(low_lanes, both[:LANES], both[LANES:]))
    return jnp.concatenate(tiles, axis=1)


def pushes(b_block, to_end, group, values, block, head_count):
    state_count = b_block.shape[0]
    groups = LANES // group
    lane = iota((state_count, LANES), 1)
    tiles = [[] for _ in range(groups)]
    for pair in range(head_count // 2):
        rows = []
        for g in range(groups):
            for head in (2 * pair, 2 * pair + 1):
                at = block * head_count + head
                coef = b_block * to_end[at : at + 1, :]
                rows.append(jnp.where(lane // group == g, coef, 0.0).astype(bf16))
        left = dot(jnp.concatenate(rows, axis=0), values[:, pair * LANES : (pair + 1) * LANES])
        for g in range(groups):
            top = left[2 * g * state_count : (2 * g + 1) * state_count]
            bottom = left[(2 * g + 1) * state_count : (2 * g + 2) * state_count]
            tiles[g].append(jnp.where(lane < LANES // 2, top, bottom))
    return [jnp.concatenate(t, axis=1) for t in tiles]


def prepare(patches, tissue, w_value, w_proj, bias, rates, masked, values, proj, b_rows, run_col, less_row, payload):
    line_count, width = tissue.shape
    head_count = bias.shape[-1]
    flags = jnp.transpose(tissue[...].astype(f32))
    for r in range(line_count):
        keep = jnp.broadcast_to(flags[:, r : r + 1], (width, patches.shape[1])).astype(bf16)
        rows = slice(r * width, (r + 1) * width)
        masked[rows, :] = patches[rows, :] * keep
    inputs = masked[...]
    narrow = dot(inputs, w_value[...]).astype(bf16)
    values[...] = narrow
    proj[...] = dot(inputs, w_proj[...])
    proj_rows = lax.dot_general(
        w_proj[...], inputs, (((0,), (1,)), ((), ())), preferred_element_type=f32
    )
    state_count = (proj.shape[1] - head_count) // 2
    b_rows[...] = proj_rows[:state_count]
    running, less, totals = step_terms(proj_rows, bias[...], rates[...], width)
    less_row[...] = less
    run_col[...] = jnp.transpose(running)
    to_end = jnp.exp(totals - less)
    total_cols = jnp.transpose(totals)
    blocks = inputs.shape[0] // LANES
    groups = LANES // width
    shape = (line_count, blocks * head_count)
    line, column = iota(shape, 0), iota(shape, 1)
    picked = jnp.zeros(shape, f32)
    for g in range(groups):
        here = (line % groups == g) & (column // head_count == line // groups)
        picked = jnp.where(here, total_cols[g * width : g * width + 1, :], picked)
    lanes = jnp.concatenate([head_lanes(head_count, inputs.shape[1] // head_count)] * blocks, axis=0)
    decays = jnp.exp(dot(picked, lanes, highest))
    high, low = halves(decays)
    high, low = high.astype(f32), low.astype(f32)
    tail = iota((8, inputs.shape[1]), 0)
    for k in range(blocks):
        at = slice(k * LANES, (k + 1) * LANES)
        left = pushes(proj_rows[:state_count, at], to_end, width, narrow[at], k, head_count)
        for g in range(groups):
            r = k * groups + g
            payload[r, :state_count, :] = left[g].astype(bf16)
            payload[r, state_count:, :] = jnp.where(
                tail == 0, high[r : r + 1], jnp.where(tail == 1, low[r : r + 1], 0.0)
            ).astype(bf16)


def spread(row, lanes):
    return dot(jnp.broadcast_to(row, (8, row.shape[-1])), lanes, highest)[:1]


def make_within(group):
    def body(values, proj, b_rows, run_col, less_row, skips, outputs):
        head_count = skips.shape[-1]
        count, width_all = values.shape
        skip = spread(skips[...], head_lanes(head_count, width_all // head_count))
        for k in range(count // LANES):
            at = slice(k * LANES, (k + 1) * LANES)
            block = values[at, :]
            own = within(
                proj[at, :], b_rows[:, at], group, run_col[...], less_row[...], block, k, head_count
            )
            outputs[at, :] = own + skip * block.astype(f32)

    return body


def enter(payload, entering):
    device_count, _, width_all = payload.shape
    state_count = entering.shape[1]
    state = jnp.zeros((state_count, width_all), f32)
    for k in range(device_count):
        entering[k] = state.astype(bf16)
        tail = payload[k, state_count:, :].astype(f32)
        decay = tail[0:1] + tail[1:2]
        state = decay * state + payload[k, :state_count, :].astype(f32)


def reach_lanes(run_col_block, block, head_count, width_all):
    shape = (run_col_block.shape[1], width_all)
    row, lane = iota(shape, 0), iota(shape, 1)
    here = (row // head_count == block) & (row % head_count == lane // (width_all // head_count))
    lanes = jnp.where(here, 1.0, 0.0).astype(bf16)
    high, low = halves(jnp.exp(run_col_block))
    return dot(high, lanes) + dot(low, lanes)


def normed(values, gain):
    square = jnp.mean(values * values, axis=-1, keepdims=True)
    return values * lax.rsqrt(square + 1e-05) * gain


def swap_matrix(count, inner):
    outer = count // inner
    place, source = iota((count, count), 0), iota((count, count), 1)
    return jnp.where((place % outer) * inner + place // outer == source, 1.0, 0.0).astype(bf16)


def finish_rows(outputs, proj, run_col, entering, gain, lines):
    line_count, state_count, width_all = entering.shape
    count = outputs.shape[0]
    width = count // line_count
    head_count = proj.shape[1] - 2 * state_count
    done = []
    for k in range(count // LANES):
        at = slice(k * LANES, (k + 1) * LANES)
        reach = reach_lanes(run_col[...], k, head_count, width_all)
        extra = []
        for r in range(k * LANES // width, (k + 1) * LANES // width):
            high, low = halves(proj[r * width : (r + 1) * width, :])
            state = jnp.concatenate(
                [
                    jnp.zeros((state_count, width_all), bf16),
                    entering[r],
                    jnp.zeros((head_count, width_all), bf16),
                ],
                axis=0,
            )
            extra.append(dot(high, state) + dot(low, state))
        whole = outputs[at, :] + jnp.concatenate(extra, axis=0) * reach
        done.append(normed(whole, gain[...]).astype(bf16))
    lines[...] = dot(swap_matrix(count, width), jnp.concatenate(done, axis=0)).astype(bf16)


def scan_columns(lines, w_proj, bias, rates, skips, outputs):
    count, width_all = lines.shape
    head_count = bias.shape[-1]
    inputs = lines[...]
    proj = dot(inputs, w_proj[...])
    proj_rows = lax.dot_general(
        w_proj[...], inputs, (((0,), (1,)), ((), ())), preferred_element_type=f32
    )
    state_count = (proj.shape[1] - head_count) // 2
    running, less, totals = step_terms(proj_rows, bias[...], rates[...], LANES)
    run_col = jnp.transpose(running)
    to_end = jnp.exp(totals - less)
    total_cols = jnp.transpose(totals)
    lanes = head_lanes(head_count, width_all // head_count)
    skip = spread(skips[...], lanes)
    blocks = count // LANES
    shape = (8, blocks * head_count)
    here = iota(shape, 1) // head_count == iota(shape, 0)
    picked = jnp.where(here, jnp.broadcast_to(total_cols[:1], shape), 0.0)
    decays = jnp.exp(dot(picked, jnp.concatenate([lanes] * blocks, axis=0), highest))
    state = jnp.zeros((state_count, width_all), f32)
    for k in range(blocks):
        at = slice(k * LANES, (k + 1) * LANES)
        block = inputs[at]
        b_block = proj_rows[:state_count, at]
        own = within(proj[at], b_block, LANES, run_col, less, block, k, head_count)
        own = own + skip * block.astype(f32)
        if k > 0:
            padded = jnp.concatenate(
                [
                    jnp.zeros((state_count, width_all), f32),
                    state,
                    jnp.zeros((head_count, width_all), f32),
                ],
                axis=0,
            )
            own = own + dot(proj[at], padded, highest) * reach_lanes(
                run_col, k, head_count, width_all
            )
        outputs[at, :] = own.astype(bf16)
        if k + 1 < blocks:
            left = pushes(b_block, to_end, LANES, block, k, head_count)[0]
            state = decays[k : k + 1] * state + left


def make_gate(width):
    def gate(masked, w_gate, gates):
        value = dot(masked[...], w_gate[...])
        gates[...] = value / (1.0 + jnp.exp(-value))

    return gate


def make_finish(width):
    def finish(columns, gates, masked, w_out, gain, mixed):
        count = columns.shape[0]
        swapped = dot(swap_matrix(count, count // width), columns[...])
        act = (normed(swapped, gain[...]) * gates[...]).astype(bf16)
        mixed[...] = (masked[...].astype(f32) + dot(act, w_out[...])).astype(bf16)

    return finish


def call(body, out_shape, *args, flops=0, name=None):
    in_place = pl.BlockSpec(memory_space=pltpu.VMEM)
    single = not isinstance(out_shape, tuple)
    return pl.pallas_call(
        body,
        out_shape=out_shape,
        in_specs=[in_place] * len(args),
        out_specs=in_place if single else tuple(in_place for _ in out_shape),
        name=name,
        cost_estimate=pl.CostEstimate(flops=flops, bytes_accessed=4 << 20, transcendentals=0),
        compiler_params=pltpu.CompilerParams(vmem_limit_bytes=24 << 20),
    )(*args)


def on_device(
    patches,
    tissue,
    w_value,
    w_across,
    w_down,
    w_gate,
    w_out,
    step_bias_across,
    step_bias_down,
    rates_across,
    rates_down,
    skip_across,
    skip_down,
    gain_across,
    gain_final,
):
    shape = jax.ShapeDtypeStruct
    line_count, width, width_all = patches.shape
    count = line_count * width
    head_count = rates_across.shape[0]
    proj_count = w_across.shape[1]
    state_count = (proj_count - head_count) // 2
    blocks = count // LANES
    row = lambda x: x.reshape(1, -1)
    masked, values, proj, b_rows, run_col, less_row, payload = call(
        prepare,
        (
            shape((count, width_all), bf16),
            shape((count, width_all), bf16),
            shape((count, proj_count), f32),
            shape((state_count, count), f32),
            shape((LANES, blocks * head_count), f32),
            shape((blocks * head_count, LANES), f32),
            shape((line_count, state_count + 8, width_all), bf16),
        ),
        patches.reshape(count, width_all),
        tissue,
        w_value,
        w_across,
        row(step_bias_across),
        row(rates_across),
        flops=5 * 10**8,
        name="prepare",
    )
    payload = lax.all_to_all(payload, "cols", 0, 0, tiled=True)
    entering = call(
        enter,
        shape((payload.shape[0], state_count, width_all), bf16),
        payload,
        flops=10**6,
        name="enter",
    )
    entering = lax.all_to_all(entering, "cols", 0, 0, tiled=True)
    outputs = call(
        make_within(width),
        shape((count, width_all), f32),
        values,
        proj,
        b_rows,
        run_col,
        less_row,
        row(skip_across),
        flops=10**9,
        name="within_rows",
    )
    gates = call(
        make_gate(width),
        shape((count, width_all), f32),
        masked,
        w_gate,
        flops=5 * 10**8,
        name="gate",
    )
    lines = call(
        finish_rows,
        shape((count, width_all), bf16),
        outputs,
        proj,
        run_col,
        entering,
        row(gain_across),
        flops=5 * 10**8,
        name="finish_rows",
    )
    split = (count // line_count, line_count, width_all)
    lines = lax.all_to_all(lines.reshape(split), "rows", 0, 0, tiled=True)
    columns = call(
        scan_columns,
        shape((count, width_all), bf16),
        lines.reshape(count, width_all),
        w_down,
        row(step_bias_down),
        row(rates_down),
        row(skip_down),
        flops=10**9,
        name="scan_columns",
    )
    columns = lax.all_to_all(columns.reshape(split), "rows", 0, 0, tiled=True)
    mixed = call(
        make_finish(width),
        shape((count, width_all), bf16),
        columns.reshape(count, width_all),
        gates,
        masked,
        w_out,
        row(gain_final),
        flops=5 * 10**8,
        name="finish",
    )
    return mixed.reshape(patches.shape)


def solution(mesh):
    return jax.shard_map(
        on_device,
        mesh=mesh,
        in_specs=(P("rows", "cols", None), P("rows", "cols")) + (P(),) * 13,
        out_specs=P("rows", "cols", None),
        check_vma=False,
    )
```

time: 171 us -> 94.7 us (0.55)
  the two profiles are of different devices: /device:TPU:18 before, /device:TPU:16 now
where the time goes in v1:
time: 94.7 us; the launch traced here: 94.1 us
  waiting for transfers between devices  41.1 us (43%)
  starting transfers between devices  25.3 us (27%)
  Pallas kernels  11.4 us (12%)
  blocking collectives  10.9 us (12%)
  local copies, waits for them, and re-layouts  5.13 us (5%)
    all_to_all x1, waiting for transfers between devices, on_device(): lines = lax.all_to_all(lines.reshape(split), 'rows', 0, 0, tiled=True)  19.1 us
    all_to_all x1, waiting for transfers between devices, on_device(): columns = lax.all_to_all(columns.reshape(split), 'rows', 0, 0, tiled=True)  18.1 us
    all_to_all x1, starting transfers between devices, on_device(): lines = lax.all_to_all(lines.reshape(split), 'rows', 0, 0, tiled=True)  16.6 us
    pallas_call x7, Pallas kernels, call(): pl.pallas_call(body, out_shape=out_shape, in_specs=[in_place] * len(args)...  11.4 us
    all_to_all x1, blocking collectives, on_device(): payload = lax.all_to_all(payload, 'cols', 0, 0, tiled=True)  10.9 us
    all_to_all x1, starting transfers between devices, on_device(): columns = lax.all_to_all(columns.reshape(split), 'rows', 0, 0, tiled=True)  5.36 us
    unnamed x30, local copies, waits for them, and re-layouts  5.13 us
    all_to_all x1, waiting for transfers between devices, on_device(): entering = lax.all_to_all(entering, 'cols', 0, 0, tiled=True)  3.93 us
  transfers between devices with their start and end apart: 3, of which 3 were waited for; matrix products, arithmetic and copies ran while one was open for 0% of the time, Pallas kernels for 2%

profile of v1, /device:TPU:16, one launch (start us, length us, event | category | flops | bytes accessed | tf_op | source)
XLA Modules:
  0.0 94.1 jit_solution(17426284296568680591)
XLA Ops:
  0.0 0.9 copy.16.w_proj
  0.9 0.0 copy-start.6
  0.9 0.7 copy-done.6
  1.6 1.0 %copy-done.4 = bf16[8,64,512]{2,1,0:T(8,128)(2,1)S(1)} copy-done((bf16[8,64,512]{2,1,0:T(8,128)(2,1)S(1)}, bf16[8,64,512]{2,1,0:T(8,128)(2,1)}, u32[]{:S(2)}) %copy-start.4) | copy-done | bytes 524312
  2.6 1.0 %copy-done.5 = bf16[512,512]{1,0:T(8,128)(2,1)S(1)} copy-done((bf16[512,512]{1,0:T(8,128)(2,1)S(1)}, bf16[512,512]{1,0:T(8,128)(2,1)}, u32[]{:S(2)}) %copy-start.5) | copy-done | bytes 524312
  3.7 1.4 %prepare.1 = (bf16[512,512]{1,0:T(8,128)(2,1)S(1)}, bf16[512,512]{1,0:T(8,128)(2,1)S(1)}, f32[512,40]{1,0:T(8,128)S(1)}, f32[16,512]{1,0:T(8,128)S(1)}, f32[128,...) custom-call(bf16[512,512]{1,0:T(8,128)(2,1)S(1)} %bitcast.18, s32[8,64]{1,0:T(8,128)S(1)} %copy-done.6, ...), custom_call_target="tpu_custom_call" | custom-call | flops 500000000 | bytes 4194304 | tf_op jit(solution)/shard_map/prepare/pallas_call | solution.py:292
  5.1 10.9 %all_to_all.20.payload = bf16[8,24,512]{2,1,0:T(8,128)(2,1)S(1)} all-to-all(bf16[8,24,512]{2,1,0:T(8,128)(2,1)S(1)} %get-tuple-element.17), channel_id=1, replica_groups=mesh['rows'=64,'cols'=8] {'cols'}, dimensions={0} | all-to-all | bytes 393216 | tf_op jit(solution)/shard_map/all_to_all | solution.py:348
  16.0 0.7 enter.1
  16.7 3.4 %all-to-all-start.1 = ((bf16[8,16,512]{2,1,0:T(8,128)(2,1)}), bf16[8,16,512]{2,1,0:T(8,128)(2,1)S(1)}, u32[]{:S(2)}, u32[]{:S(2)}) async-start(bf16[8,16,512]{2,1,0:T(8,128)(2,1)} %enter.1), calls=%async_computation.1 | async-start | bytes 262144 | tf_op jit(solution)/shard_map/all_to_all | solution.py:356
  20.1 0.6 copy-done.9
  20.8 1.5 %within_rows.1.outputs = f32[512,512]{1,0:T(8,128)S(1)} custom-call(bf16[512,512]{1,0:T(8,128)(2,1)S(1)} %get-tuple-element.12.values, f32[512,40]{1,0:T(8,128)S(1)} %get-tuple-element.13.proj, f32[16,512]{1,0:T(8,128)S(1)} %get-tuple-element.14.b_rows, f32[128,32]{1,0:T(8,128)S(1)} %get-tuple-element.15.run_col, f32[32,128]{1,0:T(8,128)S(1)} %get-tuple-element.16.less_row, ...), custom_call_target="tpu_custom_call" | custom-call | flops 1000000000 | bytes 4194304 | tf_op jit(solution)/shard_map/within_rows/pallas_call | solution.py:292
  22.2 3.9 %all-to-all-done.1.entering = bf16[8,16,512]{2,1,0:T(8,128)(2,1)S(1)} async-done(((bf16[8,16,512]{2,1,0:T(8,128)(2,1)}), bf16[8,16,512]{2,1,0:T(8,128)(2,1)S(1)}, u32[]{:S(2)}, u32[]{:S(2)}) %all-to-all-start.1) | async-done | bytes 131104 | tf_op jit(solution)/shard_map/all_to_all | solution.py:356
  26.2 1.9 %finish_rows.1 = bf16[512,512]{1,0:T(8,128)(2,1)} custom-call(f32[512,512]{1,0:T(8,128)S(1)} %within_rows.1.outputs, f32[512,40]{1,0:T(8,128)S(1)} %get-tuple-element.13.proj, f32[128,32]{1,0:T(8,128)S(1)} %get-tuple-element.15.run_col, bf16[8,16,512]{2,1,0:T(8,128)(2,1)S(1)} %all-to-all-done.1.entering, f32[1,512]{1,0:T(1,128)S(1)} %bitcast.16), custom_call_target="tpu_custom_call" | custom-call | flops 500000000 | bytes 4194304 | tf_op jit(solution)/shard_map/finish_rows/pallas_call | solution.py:292
  28.0 16.6 %all-to-all-start.2 = ((bf16[64,8,512]{2,1,0:T(8,128)(2,1)}), bf16[64,8,512]{2,1,0:T(8,128)(2,1)S(1)}, u32[]{:S(2)}, u32[]{:S(2)}) async-start(bf16[64,8,512]{2,1,0:T(8,128)(2,1)} %bitcast.5), calls=%async_computation.2 | async-start | bytes 1048576 | tf_op jit(solution)/shard_map/all_to_all | solution.py:389
  44.7 0.1 copy.17.w_proj
  44.8 19.1 %all-to-all-done.2 = bf16[64,8,512]{2,1,0:T(8,128)(2,1)S(1)} async-done(((bf16[64,8,512]{2,1,0:T(8,128)(2,1)}), bf16[64,8,512]{2,1,0:T(8,128)(2,1)S(1)}, u32[]{:S(2)}, u32[]{:S(2)}) %all-to-all-start.2) | async-done | bytes 524320 | tf_op jit(solution)/shard_map/all_to_all | solution.py:389
  63.9 0.6 copy-done.10
  64.5 0.0 copy-done.11
  64.5 0.0 copy-done.12
  64.6 3.8 %scan_columns.1 = bf16[512,512]{1,0:T(8,128)(2,1)} custom-call(bf16[512,512]{1,0:T(8,128)(2,1)S(1)} %bitcast.15, bf16[512,40]{1,0:T(8,128)(2,1)S(1)} %copy.17.w_proj, f32[1,8]{1,0:T(1,128)S(1)} %bitcast.22, f32[1,8]{1,0:T(1,128)S(1)} %bitcast.23, f32[1,8]{1,0:T(1,128)S(1)} %bitcast.24), custom_call_target="tpu_custom_call" | custom-call | flops 1000000000 | bytes 4194304 | tf_op jit(solution)/shard_map/scan_columns/pallas_call | solution.py:292
  68.3 5.4 %all-to-all-start.3 = ((bf16[64,8,512]{2,1,0:T(8,128)(2,1)}), bf16[64,8,512]{2,1,0:T(8,128)(2,1)S(1)}, u32[]{:S(2)}, u32[]{:S(2)}) async-start(bf16[64,8,512]{2,1,0:T(8,128)(2,1)} %bitcast.10), calls=%async_computation.3 | async-start | bytes 1048576 | tf_op jit(solution)/shard_map/all_to_all | solution.py:401
  73.7 0.6 gate.1.gates
  74.3 18.1 %all-to-all-done.3 = bf16[64,8,512]{2,1,0:T(8,128)(2,1)S(1)} async-done(((bf16[64,8,512]{2,1,0:T(8,128)(2,1)}), bf16[64,8,512]{2,1,0:T(8,128)(2,1)S(1)}, u32[]{:S(2)}, u32[]{:S(2)}) %all-to-all-start.3) | async-done | bytes 524320 | tf_op jit(solution)/shard_map/all_to_all | solution.py:401
  92.4 1.6 %finish.1 = bf16[512,512]{1,0:T(8,128)(2,1)} custom-call(bf16[512,512]{1,0:T(8,128)(2,1)S(1)} %bitcast.14, f32[512,512]{1,0:T(8,128)S(1)} %gate.1.gates, bf16[512,512]{1,0:T(8,128)(2,1)S(1)} %get-tuple-element.18.masked, bf16[512,512]{1,0:T(8,128)(2,1)S(1)} %copy-done.1, f32[1,512]{1,0:T(1,128)S(1)} %bitcast.17), custom_call_target="tpu_custom_call" | custom-call | flops 500000000 | bytes 4194304 | tf_op jit(solution)/shard_map/finish/pallas_call | solution.py:292
  (20 shorter events, 0.0 us)
Async XLA Ops:
  0.9 0.7 copy-start.6
  0.9 0.7 copy-start.7
  0.9 0.7 copy-start.8
  1.6 1.0 %copy-start.4 = (bf16[8,64,512]{2,1,0:T(8,128)(2,1)S(1)}, bf16[8,64,512]{2,1,0:T(8,128)(2,1)}, u32[]{:S(2)}) copy-start(bf16[8,64,512]{2,1,0:T(8,128)(2,1)} %param.15) | copy-start | bytes 1572868
  2.6 1.0 %copy-start.5 = (bf16[512,512]{1,0:T(8,128)(2,1)S(1)}, bf16[512,512]{1,0:T(8,128)(2,1)}, u32[]{:S(2)}) copy-start(bf16[512,512]{1,0:T(8,128)(2,1)} %w_value.1) | copy-start | bytes 1572868
  16.7 9.4 %all-to-all-start.1 = ((bf16[8,16,512]{2,1,0:T(8,128)(2,1)}), bf16[8,16,512]{2,1,0:T(8,128)(2,1)S(1)}, u32[]{:S(2)}, u32[]{:S(2)}) async-start(bf16[8,16,512]{2,1,0:T(8,128)(2,1)} %enter.1), calls=%async_computation.1 | async-start | bytes 262144 | tf_op jit(solution)/shard_map/all_to_all | solution.py:356
  20.1 0.7 copy-start.9
  20.8 5.4 %copy-start.2 = (f32[512]{0:T(512)S(1)}, f32[512]{0:T(512)}, u32[]{:S(2)}) copy-start(f32[512]{0:T(512)} %param.28) | copy-start | bytes 6148
  28.0 16.6 %copy-start.13 = (bf16[512,40]{0,1:T(8,128)(2,1)S(1)}, bf16[512,40]{0,1:T(8,128)(2,1)}, u32[]{:S(2)}) copy-start(bf16[512,40]{0,1:T(8,128)(2,1)} %param.19) | copy-start | bytes 122884
  28.0 35.8 %all-to-all-start.2 = ((bf16[64,8,512]{2,1,0:T(8,128)(2,1)}), bf16[64,8,512]{2,1,0:T(8,128)(2,1)S(1)}, u32[]{:S(2)}, u32[]{:S(2)}) async-start(bf16[64,8,512]{2,1,0:T(8,128)(2,1)} %bitcast.5), calls=%async_computation.2 | async-start | bytes 1048576 | tf_op jit(solution)/shard_map/all_to_all | solution.py:389
  63.9 0.7 copy-start.10
  63.9 0.7 copy-start.11
  63.9 0.7 copy-start.12
  68.3 5.4 %copy-start = (bf16[512,512]{1,0:T(8,128)(2,1)S(1)}, bf16[512,512]{1,0:T(8,128)(2,1)}, u32[]{:S(2)}) copy-start(bf16[512,512]{1,0:T(8,128)(2,1)} %w_gate.1) | copy-start | bytes 1572868
  68.3 24.1 %all-to-all-start.3 = ((bf16[64,8,512]{2,1,0:T(8,128)(2,1)}), bf16[64,8,512]{2,1,0:T(8,128)(2,1)S(1)}, u32[]{:S(2)}, u32[]{:S(2)}) async-start(bf16[64,8,512]{2,1,0:T(8,128)(2,1)} %bitcast.10), calls=%async_computation.3 | async-start | bytes 1048576 | tf_op jit(solution)/shard_map/all_to_all | solution.py:401
  73.7 18.7 %copy-start.1 = (bf16[512,512]{1,0:T(8,128)(2,1)S(1)}, bf16[512,512]{1,0:T(8,128)(2,1)}, u32[]{:S(2)}) copy-start(bf16[512,512]{1,0:T(8,128)(2,1)} %w_out.1) | copy-start | bytes 1572868
  74.3 18.1 %copy-start.3 = (f32[512]{0:T(512)S(1)}, f32[512]{0:T(512)}, u32[]{:S(2)}) copy-start(f32[512]{0:T(512)} %param.29) | copy-start | bytes 6148

commit v2 on v1

v2 whole, which is shorter than its diff:
```python
import jax
import jax.numpy as jnp
from jax import lax
from jax.experimental import pallas as pl
from jax.experimental.pallas import tpu as pltpu
from jax.sharding import PartitionSpec as P

bf16, f32 = jnp.bfloat16, jnp.float32
LANES = 128
CAP = 80.0


def iota(shape, dim):
    return lax.broadcasted_iota(jnp.int32, shape, dim)


def dot(a, b):
    return jnp.dot(a, b, preferred_element_type=f32)


def dot_t(a, b):
    return lax.dot_general(a, b, (((1,), (1,)), ((), ())), preferred_element_type=f32)


def halves(x):
    high = x.astype(bf16)
    return high, (x - high.astype(f32)).astype(bf16)


def softplus(v):
    return jnp.maximum(v, 0.0) + jnp.log1p(jnp.exp(-jnp.abs(v)))


def dot3(a, b):
    (ah, al), (bh, bl) = halves(a), halves(b)
    return dot(ah, bh) + (dot(al, bh) + dot(ah, bl))


def by_ones(a, ones):
    high, rest = a.astype(bf16), None
    rest = a - high.astype(f32)
    middle = rest.astype(bf16)
    low = (rest - middle.astype(f32)).astype(bf16)
    n = a.shape[0]
    whole = dot(jnp.concatenate([high.astype(f32), middle.astype(f32), low.astype(f32)], axis=0).astype(bf16), ones)
    return whole[:n] + (whole[n : 2 * n] + whole[2 * n :])


def as_column(row):
    n = row.shape[-1]
    square = jnp.broadcast_to(row, (n, n))
    return jnp.sum(jnp.where(iota((n, n), 0) == iota((n, n), 1), square, 0.0), axis=1, keepdims=True)


def head_lanes(head_count, width):
    shape = (head_count, head_count * width)
    return jnp.where(iota(shape, 1) // width == iota(shape, 0), 1.0, 0.0)


def step_terms(proj_rows, bias, rates, group):
    head_count = bias.shape[-1]
    steps = softplus(proj_rows[-head_count:] + as_column(bias))
    falls = -steps * as_column(rates)
    logs = jnp.log(steps)
    blocks = proj_rows.shape[1] // LANES
    stack = lambda x: jnp.concatenate([x[:, k * LANES : (k + 1) * LANES] for k in range(blocks)], axis=0)
    falls, logs = stack(falls), stack(logs)
    source, target = iota((LANES, LANES), 0), iota((LANES, LANES), 1)
    same = source // group == target // group
    running = by_ones(falls, jnp.where(same & (source <= target), 1.0, 0.0).astype(bf16))
    totals = by_ones(falls, jnp.where(same, 1.0, 0.0).astype(bf16))
    return running, running - logs, totals


def products(proj_block, b_block):
    state_count = b_block.shape[0]
    rest = proj_block.shape[1] - 2 * state_count
    padded = jnp.concatenate(
        [jnp.zeros_like(b_block), b_block, jnp.zeros((rest, b_block.shape[1]), f32)], axis=0
    )
    return dot3(proj_block, padded)


def within(proj_block, b_block, group, run_col, less_row, values, block, head_count):
    source, target = iota((LANES, LANES), 1), iota((LANES, LANES), 0)
    keep = (source // group == target // group) & (source <= target)
    inter = jnp.where(keep, products(proj_block, b_block), 0.0)
    low_lanes = iota((LANES, LANES), 1) < LANES // 2
    tiles = []
    for pair in range(head_count // 2):
        weights = []
        for head in (2 * pair, 2 * pair + 1):
            at = block * head_count + head
            spans = run_col[:, at : at + 1] - less_row[at : at + 1, :]
            weights.append((jnp.exp(jnp.minimum(spans, CAP)) * inter).astype(bf16))
        both = dot(jnp.concatenate(weights, axis=0), values[:, pair * LANES : (pair + 1) * LANES])
        tiles.append(jnp.where(low_lanes, both[:LANES], both[LANES:]))
    return jnp.concatenate(tiles, axis=1)


def pushes(b_block, to_end, group, values, block, head_count):
    state_count = b_block.shape[0]
    groups = LANES // group
    lane = iota((state_count, LANES), 1)
    tiles = [[] for _ in range(groups)]
    for pair in range(head_count // 2):
        rows = []
        for g in range(groups):
            for head in (2 * pair, 2 * pair + 1):
                at = block * head_count + head
                coef = b_block * to_end[at : at + 1, :]
                rows.append(jnp.where(lane // group == g, coef, 0.0).astype(bf16))
        left = dot(jnp.concatenate(rows, axis=0), values[:, pair * LANES : (pair + 1) * LANES])
        for g in range(groups):
            top = left[2 * g * state_count : (2 * g + 1) * state_count]
            bottom = left[(2 * g + 1) * state_count : (2 * g + 2) * state_count]
            tiles[g].append(jnp.where(lane < LANES // 2, top, bottom))
    return [jnp.concatenate(t, axis=1) for t in tiles]


def fetch(sources, targets, sems):
    copies = [
        pltpu.make_async_copy(source, target, sems.at[i])
        for i, (source, target) in enumerate(zip(sources, targets))
    ]
    for copy in copies:
        copy.start()
    return copies


def prepare(*refs):
    patches, tissue, w_value, w_proj, bias, rates = refs[:6]
    masked, values, proj, b_rows, run_col, less_row, payload = refs[6:13]
    patches_in, tissue_in, value_in, proj_in, bias_in, rates_in, sems = refs[13:]
    copies = fetch(
        (tissue, patches, w_proj, bias, rates, w_value),
        (tissue_in, patches_in, proj_in, bias_in, rates_in, value_in),
        sems,
    )
    line_count, width = tissue_in.shape
    head_count = bias_in.shape[-1]
    copies[0].wait()
    flags = jnp.transpose(tissue_in[...].astype(f32))
    copies[1].wait()
    for r in range(line_count):
        keep = jnp.broadcast_to(flags[:, r : r + 1], (width, patches_in.shape[1])).astype(bf16)
        rows = slice(r * width, (r + 1) * width)
        masked[rows, :] = patches_in[rows, :] * keep
    inputs = masked[...]
    for copy in copies[2:5]:
        copy.wait()
    proj[...] = dot_t(inputs, proj_in[...])
    proj_rows = dot_t(proj_in[...], inputs)
    state_count = (proj.shape[1] - head_count) // 2
    b_rows[...] = proj_rows[:state_count]
    running, less, totals = step_terms(proj_rows, bias_in[...], rates_in[...], width)
    less_row[...] = less
    run_col[...] = jnp.transpose(running)
    to_end = jnp.exp(totals - less)
    total_cols = jnp.transpose(totals)
    blocks = inputs.shape[0] // LANES
    groups = LANES // width
    shape = (line_count, blocks * head_count)
    line, column = iota(shape, 0), iota(shape, 1)
    picked = jnp.zeros(shape, f32)
    for g in range(groups):
        here = (line % groups == g) & (column // head_count == line // groups)
        picked = jnp.where(here, total_cols[g * width : g * width + 1, :], picked)
    lanes = jnp.concatenate([head_lanes(head_count, inputs.shape[1] // head_count)] * blocks, axis=0)
    decays = jnp.exp(by_ones(picked, lanes.astype(bf16)))
    keep_decays(payload, decays)
    copies[5].wait()
    narrow = dot(inputs, value_in[...]).astype(bf16)
    values[...] = narrow
    for k in range(blocks):
        at = slice(k * LANES, (k + 1) * LANES)
        left = pushes(proj_rows[:state_count, at], to_end, width, narrow[at], k, head_count)
        for g in range(groups):
            r = k * groups + g
            payload[r * state_count : (r + 1) * state_count, :] = left[g].astype(bf16)


def keep_decays(payload, decays):
    high, low = halves(decays)
    pair = jnp.concatenate([high.astype(f32), low.astype(f32)], axis=0).astype(bf16)
    payload[payload.shape[0] - pair.shape[0] :, :] = pair


def read_decays(payload, line_count):
    pair = payload[payload.shape[0] - 2 * line_count :, :].astype(f32)
    return pair[:line_count] + pair[line_count:]


def line_rows(r, state_count):
    return slice(r * state_count, (r + 1) * state_count)


def first_step(own, came, state, span, sent):
    line_count = span.shape[0]
    state_count = state.shape[0] // line_count
    decays, before = read_decays(own, line_count), read_decays(came, line_count)
    span[...] = before
    keep_decays(sent, decays * before)
    for r in range(line_count):
        at = line_rows(r, state_count)
        entered = came[at, :].astype(f32)
        state[at, :] = entered
        sent[at, :] = (own[at, :].astype(f32) + decays[r : r + 1] * entered).astype(bf16)


def second_step(own, came, state, span, states, spans, sent):
    line_count = span.shape[0]
    state_count = state.shape[0] // line_count
    decays, before = read_decays(own, line_count), read_decays(came, line_count)
    over = span[...]
    spans[...] = over * before
    for r in range(line_count):
        at = line_rows(r, state_count)
        entered = state[at, :] + over[r : r + 1] * came[at, :].astype(f32)
        states[at, :] = entered
        sent[at, :] = (own[at, :].astype(f32) + decays[r : r + 1] * entered).astype(bf16)


def spread(row, lanes):
    return by_ones(jnp.broadcast_to(row, (8, row.shape[-1])), lanes.astype(bf16))[:1]


def make_within(group):
    def body(values, proj, b_rows, run_col, less_row, skips, *refs):
        given, (outputs, reach), passed = refs[:5], refs[5:7], refs[7:]
        for source, target in zip(given, passed):
            target[...] = source[...]
        head_count = skips.shape[-1]
        count, width_all = values.shape
        skip = spread(skips[...], head_lanes(head_count, width_all // head_count))
        for k in range(count // LANES):
            at = slice(k * LANES, (k + 1) * LANES)
            block = values[at, :]
            own = within(
                proj[at, :], b_rows[:, at], group, run_col[...], less_row[...], block, k, head_count
            )
            outputs[at, :] = own + skip * block.astype(f32)
            reach[at, :] = reach_lanes(run_col[...], k, head_count, width_all)

    return body


def reach_lanes(run_col_block, block, head_count, width_all):
    shape = (run_col_block.shape[1], width_all)
    row, lane = iota(shape, 0), iota(shape, 1)
    here = (row // head_count == block) & (row % head_count == lane // (width_all // head_count))
    lanes = jnp.where(here, 1.0, 0.0).astype(bf16)
    high, low = halves(jnp.exp(run_col_block))
    return dot(high, lanes) + dot(low, lanes)


def normed(values, gain):
    square = jnp.mean(values * values, axis=-1, keepdims=True)
    return values * lax.rsqrt(square + 1e-05) * gain


def swap_matrix(count, inner):
    outer = count // inner
    place, source = iota((count, count), 0), iota((count, count), 1)
    return jnp.where((place % outer) * inner + place // outer == source, 1.0, 0.0).astype(bf16)


def finish_rows(outputs, reach, proj, states, spans, came, gain, swap, lines):
    line_count, width_all = spans.shape
    state_count = states.shape[0] // line_count
    count = outputs.shape[0]
    width = count // line_count
    head_count = proj.shape[1] - 2 * state_count
    done = []
    for r in range(line_count):
        at = line_rows(r, state_count)
        state = states[at, :] + spans[r : r + 1, :] * came[at, :].astype(f32)
        padded = jnp.concatenate(
            [
                jnp.zeros((state_count, width_all), f32),
                state,
                jnp.zeros((head_count, width_all), f32),
            ],
            axis=0,
        )
        rows = slice(r * width, (r + 1) * width)
        whole = outputs[rows, :] + dot3(proj[rows, :], padded) * reach[rows, :]
        done.append(normed(whole, gain[...]).astype(bf16))
    lines[...] = dot(swap[...], jnp.concatenate(done, axis=0)).astype(bf16)


def scan_columns(lines, w_proj, bias, rates, skips, outputs):
    count, width_all = lines.shape
    head_count = bias.shape[-1]
    inputs = lines[...]
    proj = dot_t(inputs, w_proj[...])
    proj_rows = dot_t(w_proj[...], inputs)
    state_count = (proj.shape[1] - head_count) // 2
    running, less, totals = step_terms(proj_rows, bias[...], rates[...], LANES)
    run_col = jnp.transpose(running)
    to_end = jnp.exp(totals - less)
    total_cols = jnp.transpose(totals)
    lanes = head_lanes(head_count, width_all // head_count)
    skip = spread(skips[...], lanes)
    blocks = count // LANES
    shape = (8, blocks * head_count)
    here = iota(shape, 1) // head_count == iota(shape, 0)
    picked = jnp.where(here, jnp.broadcast_to(total_cols[:1], shape), 0.0)
    decays = jnp.exp(by_ones(picked, jnp.concatenate([lanes] * blocks, axis=0).astype(bf16)))
    state = jnp.zeros((state_count, width_all), f32)
    for k in range(blocks):
        at = slice(k * LANES, (k + 1) * LANES)
        block = inputs[at]
        b_block = proj_rows[:state_count, at]
        own = within(proj[at], b_block, LANES, run_col, less, block, k, head_count)
        own = own + skip * block.astype(f32)
        if k > 0:
            padded = jnp.concatenate(
                [
                    jnp.zeros((state_count, width_all), f32),
                    state,
                    jnp.zeros((head_count, width_all), f32),
                ],
                axis=0,
            )
            own = own + dot3(proj[at], padded) * reach_lanes(
                run_col, k, head_count, width_all
            )
        outputs[at, :] = own.astype(bf16)
        if k + 1 < blocks:
            left = pushes(b_block, to_end, LANES, block, k, head_count)[0]
            state = decays[k : k + 1] * state + left


def make_gate(width):
    def gate(masked, w_gate, gates, swap, back):
        value = dot(masked[...], w_gate[...])
        gates[...] = value / (1.0 + jnp.exp(-value))
        count = masked.shape[0]
        swap[...] = swap_matrix(count, width)
        back[...] = swap_matrix(count, count // width)

    return gate


def finish(columns, gates, masked, w_out, gain, back, mixed, rows_out, sems):
    act = (normed(dot(back[...], columns[...]), gain[...]) * gates[...]).astype(bf16)
    copies = []
    part = mixed.shape[1] // sems.shape[0]
    for k in range(sems.shape[0]):
        at = slice(k * part, (k + 1) * part)
        rows_out[:, at] = (masked[:, at].astype(f32) + dot(act, w_out[:, at])).astype(bf16)
        copies.append(pltpu.make_async_copy(rows_out.at[:, at], mixed.at[:, at], sems.at[k]))
        copies[-1].start()
    for copy in copies:
        copy.wait()


def shifted(value, axis, by):
    count = lax.axis_size(axis)
    return lax.ppermute(value, axis, [(i, i + by) for i in range(count - by)])


IN_VMEM = pl.BlockSpec(memory_space=pltpu.VMEM)
IN_PLACE = pl.BlockSpec(memory_space=pltpu.HBM)


def call(body, out_shape, *args, flops=0, name=None, ins=IN_VMEM, outs=IN_VMEM, scratch=()):
    single = not isinstance(out_shape, tuple)
    return pl.pallas_call(
        body,
        out_shape=out_shape,
        in_specs=[ins] * len(args),
        out_specs=outs if single else tuple(outs for _ in out_shape),
        scratch_shapes=scratch,
        name=name,
        cost_estimate=pl.CostEstimate(flops=flops, bytes_accessed=4 << 20, transcendentals=0),
        compiler_params=pltpu.CompilerParams(vmem_limit_bytes=24 << 20),
    )(*args)


def on_device(
    patches,
    tissue,
    w_value,
    w_across,
    w_down,
    w_gate,
    w_out,
    step_bias_across,
    step_bias_down,
    rates_across,
    rates_down,
    skip_across,
    skip_down,
    gain_across,
    gain_final,
):
    shape = jax.ShapeDtypeStruct
    line_count, width, width_all = patches.shape
    count = line_count * width
    head_count = rates_across.shape[0]
    proj_count = w_across.shape[1]
    state_count = (proj_count - head_count) // 2
    blocks = count // LANES
    row = lambda x: x.reshape(1, -1)
    state_rows = line_count * state_count
    given = (
        patches.reshape(count, width_all),
        tissue,
        w_value,
        w_across.T,
        row(step_bias_across),
        row(rates_across),
    )
    masked, values, proj, b_rows, run_col, less_row, payload = call(
        prepare,
        (
            shape((count, width_all), bf16),
            shape((count, width_all), bf16),
            shape((count, proj_count), f32),
            shape((state_count, count), f32),
            shape((LANES, blocks * head_count), f32),
            shape((blocks * head_count, LANES), f32),
            shape((state_rows + 2 * line_count, width_all), bf16),
        ),
        *(pltpu.with_memory_space_constraint(x, pltpu.HBM) for x in given),
        flops=5 * 10**8,
        name="prepare",
        ins=IN_PLACE,
        scratch=[pltpu.VMEM(x.shape, x.dtype) for x in given]
        + [pltpu.SemaphoreType.DMA((len(given),))],
    )
    came = shifted(payload, "cols", 1)
    state, span, sent = call(
        first_step,
        (
            shape((state_rows, width_all), f32),
            shape((line_count, width_all), f32),
            shape(payload.shape, bf16),
        ),
        payload,
        came,
        flops=10**6,
        name="first_step",
    )
    came = shifted(sent, "cols", 2)
    early, _ = lax.optimization_barrier((masked, sent))
    gates, swap, back = call(
        make_gate(width),
        (
            shape((count, width_all), f32),
            shape((count, count), bf16),
            shape((count, count), bf16),
        ),
        early,
        w_gate,
        flops=5 * 10**8,
        name="gate",
    )
    came, gates = lax.optimization_barrier((came, gates))
    states, spans, sent = call(
        second_step,
        (
            shape((state_rows, width_all), f32),
            shape((line_count, width_all), f32),
            shape((state_rows, width_all), bf16),
        ),
        payload,
        came,
        state,
        span,
        flops=10**6,
        name="second_step",
    )
    came = shifted(sent, "cols", 4)
    values, _ = lax.optimization_barrier((values, sent))
    passed = tuple(
        row(x) for x in (step_bias_down, rates_down, skip_down, gain_across, gain_final)
    )
    outputs, reach, bias_down, rate_down, skips_down, gains_across, gains_final = call(
        make_within(width),
        (shape((count, width_all), f32), shape((count, width_all), f32))
        + tuple(shape(x.shape, x.dtype) for x in passed),
        values,
        proj,
        b_rows,
        run_col,
        less_row,
        row(skip_across),
        *passed,
        flops=10**9,
        name="within_rows",
    )
    lines = call(
        finish_rows,
        shape((count, width_all), bf16),
        outputs,
        reach,
        proj,
        states,
        spans,
        came,
        gains_across,
        swap,
        flops=5 * 10**8,
        name="finish_rows",
    )
    split = (count // line_count, line_count, width_all)
    lines = lax.all_to_all(lines.reshape(split), "rows", 0, 0, tiled=True)
    columns = call(
        scan_columns,
        shape((count, width_all), bf16),
        lines.reshape(count, width_all),
        w_down.T,
        bias_down,
        rate_down,
        skips_down,
        flops=10**9,
        name="scan_columns",
    )
    columns = lax.all_to_all(columns.reshape(split), "rows", 0, 0, tiled=True)
    mixed = call(
        finish,
        shape((count, width_all), bf16),
        columns.reshape(count, width_all),
        gates,
        masked,
        w_out,
        gains_final,
        back,
        flops=5 * 10**8,
        name="finish",
        outs=IN_PLACE,
        scratch=[
            pltpu.VMEM((count, width_all), bf16),
            pltpu.SemaphoreType.DMA((2,)),
        ],
    )
    return mixed.reshape(patches.shape)


def solution(mesh):
    return jax.shard_map(
        on_device,
        mesh=mesh,
        in_specs=(P("rows", "cols", None), P("rows", "cols")) + (P(),) * 13,
        out_specs=P("rows", "cols", None),
        check_vma=False,
    )
```

time: 94.7 us -> 83.8 us (0.88)
  the two profiles are of different devices: /device:TPU:16 before, /device:TPU:4 now
where the time goes in v2:
time: 83.8 us; the launch traced here: 83.5 us
  blocking collectives  53.7 us (64%)
  waiting for transfers between devices  12.4 us (15%)
  Pallas kernels  10.2 us (12%)
  starting transfers between devices  6.32 us (8%)
    all_to_all x1, blocking collectives, on_device(): lines = lax.all_to_all(lines.reshape(split), 'rows', 0, 0, tiled=True)  32.8 us
    all_to_all x1, blocking collectives, on_device(): columns = lax.all_to_all(columns.reshape(split), 'rows', 0, 0, tiled=True)  21 us
    ppermute x3, waiting for transfers between devices, shifted(): return lax.ppermute(value, axis, [(i, i + by) for i in range(count - by)])  12.4 us
    pallas_call x8, Pallas kernels, call(): pl.pallas_call(body, out_shape=out_shape, in_specs=[ins] * len(args), out...  10.2 us
    ppermute x3, starting transfers between devices, shifted(): return lax.ppermute(value, axis, [(i, i + by) for i in range(count - by)])  6.32 us
  transfers between devices with their start and end apart: 3, of which 3 were waited for; matrix products, arithmetic and copies ran while one was open for 0% of the time, Pallas kernels for 3%

profile of v2, /device:TPU:4, one launch (start us, length us, event | category | flops | bytes accessed | tf_op | source)
XLA Modules:
  0.0 83.5 jit_solution(14983408423971652561)
XLA Ops:
  0.0 2.6 %prepare.1 = (bf16[512,512]{1,0:T(8,128)(2,1)S(1)}, bf16[512,512]{1,0:T(8,128)(2,1)S(1)}, f32[512,40]{1,0:T(8,128)S(1)}, f32[16,512]{1,0:T(8,128)S(1)}, f32[128,...) custom-call(bf16[512,512]{1,0:T(8,128)(2,1)} %bitcast.27, s32[8,64]{1,0:T(8,128)} %refs_1_.1, ...), custom_call_target="tpu_custom_call" | custom-call | flops 500000000 | bytes 4194304 | tf_op jit(solution)/shard_map/prepare/pallas_call | solution.py:370
  2.7 1.9 %collective-permute-start = (bf16[144,512]{1,0:T(8,128)(2,1)S(1)}, bf16[144,512]{1,0:T(8,128)(2,1)S(1)}, u32[]{:S(2)}, u32[]{:S(2)}) collective-permute-start(bf16[144,512]{1,0:T(8,128)(2,1)S(1)} %get-tuple-element.33.own), channel_id=1, source_target_pairs={{0,1},{1,2},{2,3},{3,4},{4,5},{5,6},{6,7},{8,9},{9,10},{10,11},{11... | collective-permute-start | bytes 442376 | tf_op jit(solution)/shard_map/ppermute | solution.py:361
  4.6 4.5 %collective-permute-done.came = bf16[144,512]{1,0:T(8,128)(2,1)S(1)} collective-permute-done((bf16[144,512]{1,0:T(8,128)(2,1)S(1)}, bf16[144,512]{1,0:T(8,128)(2,1)S(1)}, u32[]{:S(2)}, u32[]{:S(2)}) %collective-permute-start) | collective-permute-done | bytes 147488 | tf_op jit(solution)/shard_map/ppermute | solution.py:361
  9.1 0.1 first_step.1
  9.2 3.1 %collective-permute-start.1 = (bf16[144,512]{1,0:T(8,128)(2,1)S(1)}, bf16[144,512]{1,0:T(8,128)(2,1)S(1)}, u32[]{:S(2)}, u32[]{:S(2)}) collective-permute-start(bf16[144,512]{1,0:T(8,128)(2,1)S(1)} %get-tuple-element.34), channel_id=1, source_target_pairs={{0,2},{1,3},{2,4},{3,5},{4,6},{5,7},{8,10},{9,11},{10,12},{11,13},... | collective-permute-start | bytes 442376 | tf_op jit(solution)/shard_map/ppermute | solution.py:361
  12.3 1.1 %gate.1 = (f32[512,512]{1,0:T(8,128)S(1)}, bf16[512,512]{1,0:T(8,128)(2,1)S(1)}, bf16[512,512]{1,0:T(8,128)(2,1)S(1)}) custom-call(bf16[512,512]{1,0:T(8,128)(2,1)S(1)} %get-tuple-element.36.masked, bf16[512,512]{1,0:T(8,128)(2,1)S(1)} %copy-done.1), custom_call_target="tpu_custom_call" | custom-call | flops 500000000 | bytes 4194304 | tf_op jit(solution)/shard_map/gate/pallas_call | solution.py:370
  13.4 2.9 %collective-permute-done.1.came = bf16[144,512]{1,0:T(8,128)(2,1)S(1)} collective-permute-done((bf16[144,512]{1,0:T(8,128)(2,1)S(1)}, bf16[144,512]{1,0:T(8,128)(2,1)S(1)}, u32[]{:S(2)}, u32[]{:S(2)}) %collective-permute-start.1) | collective-permute-done | bytes 147488 | tf_op jit(solution)/shard_map/ppermute | solution.py:361
  16.2 0.1 second_step.1
  16.3 1.3 %collective-permute-start.2 = (bf16[128,512]{1,0:T(8,128)(2,1)S(1)}, bf16[128,512]{1,0:T(8,128)(2,1)S(1)}, u32[]{:S(2)}, u32[]{:S(2)}) collective-permute-start(bf16[128,512]{1,0:T(8,128)(2,1)S(1)} %get-tuple-element.41), channel_id=1, source_target_pairs={{0,4},{1,5},{2,6},{3,7},{8,12},{9,13},{10,14},{11,15},{16,20},{17,... | collective-permute-start | bytes 393224 | tf_op jit(solution)/shard_map/ppermute | solution.py:361
  17.6 0.0 copy-start.3
  17.6 0.0 copy-start.5
  17.6 0.0 copy-start.6
  17.6 0.0 copy-start.7
  17.7 0.6 copy-done.3
  18.3 0.0 copy-done.7
  18.3 1.4 %within_rows.1 = (f32[512,512]{1,0:T(8,128)S(1)}, f32[512,512]{1,0:T(8,128)S(1)}, f32[1,8]{1,0:T(1,128)S(1)}, f32[1,8]{1,0:T(1,128)S(1)}, f32[1,8]{1,0:T(1,128)S...) custom-call(bf16[512,512]{1,0:T(8,128)(2,1)S(1)} %get-tuple-element.42.values, f32[512,40]{1,0:T(8,128)S(1)} %get-tuple-element.43.proj, ...), custom_call_target="tpu_custom_call" | custom-call | flops 1000000000 | bytes 4194304 | tf_op jit(solution)/shard_map/within_rows/pallas_call | solution.py:370
  19.7 5.0 %collective-permute-done.2.came = bf16[128,512]{1,0:T(8,128)(2,1)S(1)} collective-permute-done((bf16[128,512]{1,0:T(8,128)(2,1)S(1)}, bf16[128,512]{1,0:T(8,128)(2,1)S(1)}, u32[]{:S(2)}, u32[]{:S(2)}) %collective-permute-start.2) | collective-permute-done | bytes 131104 | tf_op jit(solution)/shard_map/ppermute | solution.py:361
  24.7 1.0 %finish_rows.1 = bf16[512,512]{1,0:T(8,128)(2,1)S(1)} custom-call(f32[512,512]{1,0:T(8,128)S(1)} %get-tuple-element.47.outputs, f32[512,512]{1,0:T(8,128)S(1)} %get-tuple-element.48.reach, f32[512,40]{1,0:T(8,128)S(1)} %get-tuple-element.43.proj, f32[128,512]{1,0:T(8,128)S(1)} %get-tuple-element.49.states, f32[8,512]{1,0:T(8,128)S(1)} %get-tuple-element.50.spans, ...), custom_call_target="tpu_custom_call" | custom-call | flops 500000000 | bytes 4194304 | tf_op jit(solution)/shard_map/finish_rows/pallas_call | solution.py:370
  25.6 0.0 copy-start.2
  25.6 32.8 %all_to_all.10 = bf16[64,8,512]{2,1,0:T(8,128)(2,1)S(1)} all-to-all(bf16[64,8,512]{2,1,0:T(8,128)(2,1)S(1)} %bitcast.16), channel_id=1, replica_groups=mesh['rows'=64,'cols'=8] {'rows'}, dimensions={0} | all-to-all | bytes 1048576 | tf_op jit(solution)/shard_map/all_to_all | solution.py:510
  58.4 2.4 %scan_columns.1 = bf16[512,512]{1,0:T(8,128)(2,1)S(1)} custom-call(bf16[512,512]{1,0:T(8,128)(2,1)S(1)} %bitcast.18, bf16[40,512]{1,0:T(8,128)(2,1)S(1)} %bitcast.20, f32[1,8]{1,0:T(1,128)S(1)} %get-tuple-element.53.bias, f32[1,8]{1,0:T(1,128)S(1)} %get-tuple-element.54.rates, f32[1,8]{1,0:T(1,128)S(1)} %get-tuple-element.55.skips), custom_call_target="tpu_custom_call" | custom-call | flops 1000000000 | bytes 4194304 | tf_op jit(solution)/shard_map/scan_columns/pallas_call | solution.py:370
  60.8 0.0 copy-start
  60.8 21.0 %all_to_all.11 = bf16[64,8,512]{2,1,0:T(8,128)(2,1)S(1)} all-to-all(bf16[64,8,512]{2,1,0:T(8,128)(2,1)S(1)} %bitcast.19), channel_id=1, replica_groups=mesh['rows'=64,'cols'=8] {'rows'}, dimensions={0} | all-to-all | bytes 1048576 | tf_op jit(solution)/shard_map/all_to_all | solution.py:522
  81.8 1.7 %finish.1 = bf16[512,512]{1,0:T(8,128)(2,1)} custom-call(bf16[512,512]{1,0:T(8,128)(2,1)S(1)} %bitcast.17, f32[512,512]{1,0:T(8,128)S(1)} %get-tuple-element.56.gates, bf16[512,512]{1,0:T(8,128)(2,1)S(1)} %get-tuple-element.36.masked, bf16[512,512]{1,0:T(8,128)(2,1)S(1)} %copy-done, f32[1,512]{1,0:T(1,128)S(1)} %get-tuple-element.57.gain, ...), custom_call_target="tpu_custom_call" | custom-call | flops 500000000 | bytes 4194304 | tf_op jit(solution)/shard_map/finish/pallas_call | solution.py:370
  (10 shorter events, 0.0 us)
Async XLA Ops:
  0.0 12.3 %copy-start.1 = (bf16[512,512]{1,0:T(8,128)(2,1)S(1)}, bf16[512,512]{1,0:T(8,128)(2,1)}, u32[]{:S(2)}) copy-start(bf16[512,512]{1,0:T(8,128)(2,1)} %w_gate.1) | copy-start | bytes 1572868
  2.7 6.5 %collective-permute-start = (bf16[144,512]{1,0:T(8,128)(2,1)S(1)}, bf16[144,512]{1,0:T(8,128)(2,1)S(1)}, u32[]{:S(2)}, u32[]{:S(2)}) collective-permute-start(bf16[144,512]{1,0:T(8,128)(2,1)S(1)} %get-tuple-element.33.own), channel_id=1, source_target_pairs={{0,1},{1,2},{2,3},{3,4},{4,5},{5,6},{6,7},{8,9},{9,10},{10,11},{11... | collective-permute-start | bytes 442376 | tf_op jit(solution)/shard_map/ppermute | solution.py:361
  9.2 7.0 %collective-permute-start.1 = (bf16[144,512]{1,0:T(8,128)(2,1)S(1)}, bf16[144,512]{1,0:T(8,128)(2,1)S(1)}, u32[]{:S(2)}, u32[]{:S(2)}) collective-permute-start(bf16[144,512]{1,0:T(8,128)(2,1)S(1)} %get-tuple-element.34), channel_id=1, source_target_pairs={{0,2},{1,3},{2,4},{3,5},{4,6},{5,7},{8,10},{9,11},{10,12},{11,13},... | collective-permute-start | bytes 442376 | tf_op jit(solution)/shard_map/ppermute | solution.py:361
  16.2 1.4 %copy-start.4 = (f32[512]{0:T(512)S(1)}, f32[512]{0:T(512)}, u32[]{:S(2)}) copy-start(f32[512]{0:T(512)} %param.29) | copy-start | bytes 6148
  16.2 1.4 %copy-start.8 = (f32[8]{0:T(128)S(1)}, f32[8]{0:T(128)}, u32[]{:S(2)}) copy-start(f32[8]{0:T(128)} %param.27) | copy-start | bytes 100
  16.3 8.4 %collective-permute-start.2 = (bf16[128,512]{1,0:T(8,128)(2,1)S(1)}, bf16[128,512]{1,0:T(8,128)(2,1)S(1)}, u32[]{:S(2)}, u32[]{:S(2)}) collective-permute-start(bf16[128,512]{1,0:T(8,128)(2,1)S(1)} %get-tuple-element.41), channel_id=1, source_target_pairs={{0,4},{1,5},{2,6},{3,7},{8,12},{9,13},{10,14},{11,15},{16,20},{17,... | collective-permute-start | bytes 393224 | tf_op jit(solution)/shard_map/ppermute | solution.py:361
  17.6 0.7 copy-start.3
  17.6 0.7 copy-start.5
  17.6 0.7 copy-start.6
  17.6 0.7 copy-start.7
  25.6 32.8 %copy-start.2 = (bf16[512,40]{0,1:T(8,128)(2,1)S(1)}, bf16[512,40]{0,1:T(8,128)(2,1)}, u32[]{:S(2)}) copy-start(bf16[512,40]{0,1:T(8,128)(2,1)} %param.19) | copy-start | bytes 122884
  60.8 21.0 %copy-start = (bf16[512,512]{1,0:T(8,128)(2,1)S(1)}, bf16[512,512]{1,0:T(8,128)(2,1)}, u32[]{:S(2)}) copy-start(bf16[512,512]{1,0:T(8,128)(2,1)} %w_out.1) | copy-start | bytes 1572868

commit v3 on v2

--- a/solution.py
+++ b/solution.py
@@ -1,3 +1,5 @@
+import functools
+
 import jax
 import jax.numpy as jnp
 from jax import lax
@@ -8,6 +10,8 @@
 bf16, f32 = jnp.bfloat16, jnp.float32
 LANES = 128
 CAP = 80.0
+FIRST_DOWN = 46
+FIRST_BACK = 46
 
 
 def iota(shape, dim):
@@ -259,10 +263,10 @@
     return values * lax.rsqrt(square + 1e-05) * gain
 
 
-def swap_matrix(count, inner):
+def swap_matrix(count, inner, turn=0):
     outer = count // inner
     place, source = iota((count, count), 0), iota((count, count), 1)
-    return jnp.where((place % outer) * inner + place // outer == source, 1.0, 0.0).astype(bf16)
+    return jnp.where(((place + turn) % outer) * inner + place // outer == source, 1.0, 0.0).astype(bf16)
 
 
 def finish_rows(outputs, reach, proj, states, spans, came, gain, swap, lines):
@@ -289,10 +293,20 @@
     lines[...] = dot(swap[...], jnp.concatenate(done, axis=0)).astype(bf16)
 
 
-def scan_columns(lines, w_proj, bias, rates, skips, outputs):
+def put_turned(ref, start, rows):
+    count, here = ref.shape[0], start % ref.shape[0]
+    fits = min(count - here, rows.shape[0])
+    ref[here : here + fits, :] = rows[:fits]
+    if fits < rows.shape[0]:
+        ref[: rows.shape[0] - fits, :] = rows[fits:]
+
+
+def scan_columns(first, last, lines, w_proj, bias, rates, skips, outputs):
     count, width_all = lines.shape
     head_count = bias.shape[-1]
     inputs = lines[...]
+    if first:
+        inputs = jnp.concatenate([inputs[count - first :], inputs[: count - first]], axis=0)
     proj = dot_t(inputs, w_proj[...])
     proj_rows = dot_t(w_proj[...], inputs)
     state_count = (proj.shape[1] - head_count) // 2
@@ -326,19 +340,19 @@
             own = own + dot3(proj[at], padded) * reach_lanes(
                 run_col, k, head_count, width_all
             )
-        outputs[at, :] = own.astype(bf16)
+        put_turned(outputs, k * LANES - last, own.astype(bf16))
         if k + 1 < blocks:
             left = pushes(b_block, to_end, LANES, block, k, head_count)[0]
             state = decays[k : k + 1] * state + left
 
 
-def make_gate(width):
+def make_gate(width, turn):
     def gate(masked, w_gate, gates, swap, back):
         value = dot(masked[...], w_gate[...])
         gates[...] = value / (1.0 + jnp.exp(-value))
         count = masked.shape[0]
         swap[...] = swap_matrix(count, width)
-        back[...] = swap_matrix(count, count // width)
+        back[...] = swap_matrix(count, count // width, turn)
 
     return gate
 
@@ -447,7 +461,7 @@
     came = shifted(sent, "cols", 2)
     early, _ = lax.optimization_barrier((masked, sent))
     gates, swap, back = call(
-        make_gate(width),
+        make_gate(width, FIRST_DOWN - FIRST_BACK + width),
         (
             shape((count, width_all), f32),
             shape((count, count), bf16),
@@ -507,9 +521,14 @@
         name="finish_rows",
     )
     split = (count // line_count, line_count, width_all)
-    lines = lax.all_to_all(lines.reshape(split), "rows", 0, 0, tiled=True)
+    bands = lax.axis_size("rows")
+    order = lambda first: [[(i + first) % bands for i in range(bands)]]
+    exchange = lambda x, first: lax.all_to_all(
+        x.reshape(split), "rows", 0, 0, axis_index_groups=order(first), tiled=True
+    )
+    lines = exchange(lines, FIRST_DOWN)
     columns = call(
-        scan_columns,
+        functools.partial(scan_columns, FIRST_DOWN * line_count, FIRST_BACK * line_count),
         shape((count, width_all), bf16),
         lines.reshape(count, width_all),
         w_down.T,
@@ -519,7 +538,7 @@
         flops=10**9,
         name="scan_columns",
     )
-    columns = lax.all_to_all(columns.reshape(split), "rows", 0, 0, tiled=True)
+    columns = exchange(columns, FIRST_BACK)
     mixed = call(
         finish,
         shape((count, width_all), bf16),

time: 83.8 us -> 79.1 us (0.944)
  blocking collectives: 53.7 us -> 49 us
    all_to_all x2, blocking collectives: 53.7 us -> 49 us  [on_device(): lax.all_to_all(x.reshape(split), 'rows', 0, 0, axis_index_groups=order(fi...]
where the time goes in v3:
time: 79.1 us; the launch traced here: 78.7 us
  blocking collectives  49 us (62%)
  waiting for transfers between devices  12.3 us (16%)
  Pallas kernels  10.2 us (13%)
  starting transfers between devices  6.32 us (8%)
    all_to_all x2, blocking collectives, on_device(): lax.all_to_all(x.reshape(split), 'rows', 0, 0, axis_index_groups=order(fi...  49 us
    ppermute x3, waiting for transfers between devices, shifted(): return lax.ppermute(value, axis, [(i, i + by) for i in range(count - by)])  12.3 us
    pallas_call x8, Pallas kernels, call(): pl.pallas_call(body, out_shape=out_shape, in_specs=[ins] * len(args), out...  10.2 us
    ppermute x3, starting transfers between devices, shifted(): return lax.ppermute(value, axis, [(i, i + by) for i in range(count - by)])  6.32 us
  transfers between devices with their start and end apart: 3, of which 3 were waited for; matrix products, arithmetic and copies ran while one was open for 0% of the time, Pallas kernels for 3%

profile of v3, /device:TPU:4, one launch (start us, length us, event | category | flops | bytes accessed | tf_op | source)
XLA Modules:
  0.0 78.7 jit_solution(3452113067923203300)
XLA Ops:
  0.0 2.6 %prepare.1 = (bf16[512,512]{1,0:T(8,128)(2,1)S(1)}, bf16[512,512]{1,0:T(8,128)(2,1)S(1)}, f32[512,40]{1,0:T(8,128)S(1)}, f32[16,512]{1,0:T(8,128)S(1)}, f32[128,...) custom-call(bf16[512,512]{1,0:T(8,128)(2,1)} %bitcast.27, s32[8,64]{1,0:T(8,128)} %refs_1_.1, ...), custom_call_target="tpu_custom_call" | custom-call | flops 500000000 | bytes 4194304 | tf_op jit(solution)/shard_map/prepare/pallas_call | solution.py:384
  2.7 1.9 %collective-permute-start = (bf16[144,512]{1,0:T(8,128)(2,1)S(1)}, bf16[144,512]{1,0:T(8,128)(2,1)S(1)}, u32[]{:S(2)}, u32[]{:S(2)}) collective-permute-start(bf16[144,512]{1,0:T(8,128)(2,1)S(1)} %get-tuple-element.33.own), channel_id=1, source_target_pairs={{0,1},{1,2},{2,3},{3,4},{4,5},{5,6},{6,7},{8,9},{9,10},{10,11},{11... | collective-permute-start | bytes 442376 | tf_op jit(solution)/shard_map/ppermute | solution.py:375
  4.6 4.5 %collective-permute-done.came = bf16[144,512]{1,0:T(8,128)(2,1)S(1)} collective-permute-done((bf16[144,512]{1,0:T(8,128)(2,1)S(1)}, bf16[144,512]{1,0:T(8,128)(2,1)S(1)}, u32[]{:S(2)}, u32[]{:S(2)}) %collective-permute-start) | collective-permute-done | bytes 147488 | tf_op jit(solution)/shard_map/ppermute | solution.py:375
  9.1 0.1 first_step.1
  9.2 3.1 %collective-permute-start.1 = (bf16[144,512]{1,0:T(8,128)(2,1)S(1)}, bf16[144,512]{1,0:T(8,128)(2,1)S(1)}, u32[]{:S(2)}, u32[]{:S(2)}) collective-permute-start(bf16[144,512]{1,0:T(8,128)(2,1)S(1)} %get-tuple-element.34), channel_id=1, source_target_pairs={{0,2},{1,3},{2,4},{3,5},{4,6},{5,7},{8,10},{9,11},{10,12},{11,13},... | collective-permute-start | bytes 442376 | tf_op jit(solution)/shard_map/ppermute | solution.py:375
  12.3 1.1 %gate.1 = (f32[512,512]{1,0:T(8,128)S(1)}, bf16[512,512]{1,0:T(8,128)(2,1)S(1)}, bf16[512,512]{1,0:T(8,128)(2,1)S(1)}) custom-call(bf16[512,512]{1,0:T(8,128)(2,1)S(1)} %get-tuple-element.36.masked, bf16[512,512]{1,0:T(8,128)(2,1)S(1)} %copy-done.1), custom_call_target="tpu_custom_call" | custom-call | flops 500000000 | bytes 4194304 | tf_op jit(solution)/shard_map/gate/pallas_call | solution.py:384
  13.4 2.8 %collective-permute-done.1.came = bf16[144,512]{1,0:T(8,128)(2,1)S(1)} collective-permute-done((bf16[144,512]{1,0:T(8,128)(2,1)S(1)}, bf16[144,512]{1,0:T(8,128)(2,1)S(1)}, u32[]{:S(2)}, u32[]{:S(2)}) %collective-permute-start.1) | collective-permute-done | bytes 147488 | tf_op jit(solution)/shard_map/ppermute | solution.py:375
  16.2 0.1 second_step.1
  16.3 1.3 %collective-permute-start.2 = (bf16[128,512]{1,0:T(8,128)(2,1)S(1)}, bf16[128,512]{1,0:T(8,128)(2,1)S(1)}, u32[]{:S(2)}, u32[]{:S(2)}) collective-permute-start(bf16[128,512]{1,0:T(8,128)(2,1)S(1)} %get-tuple-element.41), channel_id=1, source_target_pairs={{0,4},{1,5},{2,6},{3,7},{8,12},{9,13},{10,14},{11,15},{16,20},{17,... | collective-permute-start | bytes 393224 | tf_op jit(solution)/shard_map/ppermute | solution.py:375
  17.6 0.0 copy-start.3
  17.6 0.0 copy-start.5
  17.6 0.0 copy-start.6
  17.6 0.0 copy-start.7
  17.7 0.6 copy-done.3
  18.3 0.0 copy-done.7
  18.3 1.4 %within_rows.1 = (f32[512,512]{1,0:T(8,128)S(1)}, f32[512,512]{1,0:T(8,128)S(1)}, f32[1,8]{1,0:T(1,128)S(1)}, f32[1,8]{1,0:T(1,128)S(1)}, f32[1,8]{1,0:T(1,128)S...) custom-call(bf16[512,512]{1,0:T(8,128)(2,1)S(1)} %get-tuple-element.42.values, f32[512,40]{1,0:T(8,128)S(1)} %get-tuple-element.43.proj, ...), custom_call_target="tpu_custom_call" | custom-call | flops 1000000000 | bytes 4194304 | tf_op jit(solution)/shard_map/within_rows/pallas_call | solution.py:384
  19.7 5.0 %collective-permute-done.2.came = bf16[128,512]{1,0:T(8,128)(2,1)S(1)} collective-permute-done((bf16[128,512]{1,0:T(8,128)(2,1)S(1)}, bf16[128,512]{1,0:T(8,128)(2,1)S(1)}, u32[]{:S(2)}, u32[]{:S(2)}) %collective-permute-start.2) | collective-permute-done | bytes 131104 | tf_op jit(solution)/shard_map/ppermute | solution.py:375
  24.7 1.0 %finish_rows.1 = bf16[512,512]{1,0:T(8,128)(2,1)S(1)} custom-call(f32[512,512]{1,0:T(8,128)S(1)} %get-tuple-element.47.outputs, f32[512,512]{1,0:T(8,128)S(1)} %get-tuple-element.48.reach, f32[512,40]{1,0:T(8,128)S(1)} %get-tuple-element.43.proj, f32[128,512]{1,0:T(8,128)S(1)} %get-tuple-element.49.states, f32[8,512]{1,0:T(8,128)S(1)} %get-tuple-element.50.spans, ...), custom_call_target="tpu_custom_call" | custom-call | flops 500000000 | bytes 4194304 | tf_op jit(solution)/shard_map/finish_rows/pallas_call | solution.py:384
  25.6 0.0 copy-start.2
  25.6 28.3 %all_to_all.10 = bf16[64,8,512]{2,1,0:T(8,128)(2,1)S(1)} all-to-all(bf16[64,8,512]{2,1,0:T(8,128)(2,1)S(1)} %bitcast.16), channel_id=1, replica_groups={{368,376,384,392,400,408,416,424,432,440,448,456,464,472,480,488,496,50..., dimensions={0} | all-to-all | bytes 1048576 | tf_op jit(solution)/shard_map/all_to_all | solution.py:526
  53.9 2.4 %scan_columns.1 = bf16[512,512]{1,0:T(8,128)(2,1)S(1)} custom-call(bf16[512,512]{1,0:T(8,128)(2,1)S(1)} %bitcast.18, bf16[40,512]{1,0:T(8,128)(2,1)S(1)} %bitcast.20, f32[1,8]{1,0:T(1,128)S(1)} %get-tuple-element.53.bias, f32[1,8]{1,0:T(1,128)S(1)} %get-tuple-element.54.rates, f32[1,8]{1,0:T(1,128)S(1)} %get-tuple-element.55.skips), custom_call_target="tpu_custom_call" | custom-call | flops 1000000000 | bytes 4194304 | tf_op jit(solution)/shard_map/scan_columns/pallas_call | solution.py:384
  56.3 0.0 copy-start
  56.4 20.7 %all_to_all.11 = bf16[64,8,512]{2,1,0:T(8,128)(2,1)S(1)} all-to-all(bf16[64,8,512]{2,1,0:T(8,128)(2,1)S(1)} %bitcast.19), channel_id=1, replica_groups={{368,376,384,392,400,408,416,424,432,440,448,456,464,472,480,488,496,50..., dimensions={0} | all-to-all | bytes 1048576 | tf_op jit(solution)/shard_map/all_to_all | solution.py:526
  77.1 1.7 %finish.1 = bf16[512,512]{1,0:T(8,128)(2,1)} custom-call(bf16[512,512]{1,0:T(8,128)(2,1)S(1)} %bitcast.17, f32[512,512]{1,0:T(8,128)S(1)} %get-tuple-element.56.gates, bf16[512,512]{1,0:T(8,128)(2,1)S(1)} %get-tuple-element.36.masked, bf16[512,512]{1,0:T(8,128)(2,1)S(1)} %copy-done, f32[1,512]{1,0:T(1,128)S(1)} %get-tuple-element.57.gain, ...), custom_call_target="tpu_custom_call" | custom-call | flops 500000000 | bytes 4194304 | tf_op jit(solution)/shard_map/finish/pallas_call | solution.py:384
  (10 shorter events, 0.0 us)
Async XLA Ops:
  0.0 12.3 %copy-start.1 = (bf16[512,512]{1,0:T(8,128)(2,1)S(1)}, bf16[512,512]{1,0:T(8,128)(2,1)}, u32[]{:S(2)}) copy-start(bf16[512,512]{1,0:T(8,128)(2,1)} %w_gate.1) | copy-start | bytes 1572868
  2.7 6.5 %collective-permute-start = (bf16[144,512]{1,0:T(8,128)(2,1)S(1)}, bf16[144,512]{1,0:T(8,128)(2,1)S(1)}, u32[]{:S(2)}, u32[]{:S(2)}) collective-permute-start(bf16[144,512]{1,0:T(8,128)(2,1)S(1)} %get-tuple-element.33.own), channel_id=1, source_target_pairs={{0,1},{1,2},{2,3},{3,4},{4,5},{5,6},{6,7},{8,9},{9,10},{10,11},{11... | collective-permute-start | bytes 442376 | tf_op jit(solution)/shard_map/ppermute | solution.py:375
  9.2 7.0 %collective-permute-start.1 = (bf16[144,512]{1,0:T(8,128)(2,1)S(1)}, bf16[144,512]{1,0:T(8,128)(2,1)S(1)}, u32[]{:S(2)}, u32[]{:S(2)}) collective-permute-start(bf16[144,512]{1,0:T(8,128)(2,1)S(1)} %get-tuple-element.34), channel_id=1, source_target_pairs={{0,2},{1,3},{2,4},{3,5},{4,6},{5,7},{8,10},{9,11},{10,12},{11,13},... | collective-permute-start | bytes 442376 | tf_op jit(solution)/shard_map/ppermute | solution.py:375
  16.2 1.4 %copy-start.4 = (f32[512]{0:T(512)S(1)}, f32[512]{0:T(512)}, u32[]{:S(2)}) copy-start(f32[512]{0:T(512)} %param.29) | copy-start | bytes 6148
  16.2 1.4 %copy-start.8 = (f32[8]{0:T(128)S(1)}, f32[8]{0:T(128)}, u32[]{:S(2)}) copy-start(f32[8]{0:T(128)} %param.27) | copy-start | bytes 100
  16.3 8.4 %collective-permute-start.2 = (bf16[128,512]{1,0:T(8,128)(2,1)S(1)}, bf16[128,512]{1,0:T(8,128)(2,1)S(1)}, u32[]{:S(2)}, u32[]{:S(2)}) collective-permute-start(bf16[128,512]{1,0:T(8,128)(2,1)S(1)} %get-tuple-element.41), channel_id=1, source_target_pairs={{0,4},{1,5},{2,6},{3,7},{8,12},{9,13},{10,14},{11,15},{16,20},{17,... | collective-permute-start | bytes 393224 | tf_op jit(solution)/shard_map/ppermute | solution.py:375
  17.6 0.7 copy-start.3
  17.6 0.7 copy-start.5
  17.6 0.7 copy-start.6
  17.6 0.7 copy-start.7
  25.6 28.3 %copy-start.2 = (bf16[512,40]{0,1:T(8,128)(2,1)S(1)}, bf16[512,40]{0,1:T(8,128)(2,1)}, u32[]{:S(2)}) copy-start(bf16[512,40]{0,1:T(8,128)(2,1)} %param.19) | copy-start | bytes 122884
  56.3 20.7 %copy-start = (bf16[512,512]{1,0:T(8,128)(2,1)S(1)}, bf16[512,512]{1,0:T(8,128)(2,1)}, u32[]{:S(2)}) copy-start(bf16[512,512]{1,0:T(8,128)(2,1)} %w_out.1) | copy-start | bytes 1572868

commit v4 on v3

--- a/solution.py
+++ b/solution.py
@@ -134,8 +134,8 @@
 
 def prepare(*refs):
     patches, tissue, w_value, w_proj, bias, rates = refs[:6]
-    masked, values, proj, b_rows, run_col, less_row, payload = refs[6:13]
-    patches_in, tissue_in, value_in, proj_in, bias_in, rates_in, sems = refs[13:]
+    masked, values, b_rows, run_row, less_row, payload = refs[6:12]
+    patches_in, tissue_in, value_in, proj_in, bias_in, rates_in, sems = refs[12:]
     copies = fetch(
         (tissue, patches, w_proj, bias, rates, w_value),
         (tissue_in, patches_in, proj_in, bias_in, rates_in, value_in),
@@ -153,13 +153,12 @@
     inputs = masked[...]
     for copy in copies[2:5]:
         copy.wait()
-    proj[...] = dot_t(inputs, proj_in[...])
     proj_rows = dot_t(proj_in[...], inputs)
-    state_count = (proj.shape[1] - head_count) // 2
+    state_count = b_rows.shape[0]
     b_rows[...] = proj_rows[:state_count]
     running, less, totals = step_terms(proj_rows, bias_in[...], rates_in[...], width)
     less_row[...] = less
-    run_col[...] = jnp.transpose(running)
+    run_row[...] = running
     to_end = jnp.exp(totals - less)
     total_cols = jnp.transpose(totals)
     blocks = inputs.shape[0] // LANES
@@ -230,8 +229,9 @@
 
 
 def make_within(group):
-    def body(values, proj, b_rows, run_col, less_row, skips, *refs):
-        given, (outputs, reach), passed = refs[:5], refs[5:7], refs[7:]
+    def body(values, proj, b_rows, run_row, less_row, skips, *refs):
+        given, (outputs, reach), passed = refs[:4], refs[4:6], refs[6:]
+        run_col = jnp.transpose(run_row[...])
         for source, target in zip(given, passed):
             target[...] = source[...]
         head_count = skips.shape[-1]
@@ -241,10 +241,10 @@
             at = slice(k * LANES, (k + 1) * LANES)
             block = values[at, :]
             own = within(
-                proj[at, :], b_rows[:, at], group, run_col[...], less_row[...], block, k, head_count
+                proj[at, :], b_rows[:, at], group, run_col, less_row[...], block, k, head_count
             )
             outputs[at, :] = own + skip * block.astype(f32)
-            reach[at, :] = reach_lanes(run_col[...], k, head_count, width_all)
+            reach[at, :] = reach_lanes(run_col, k, head_count, width_all)
 
     return body
 
@@ -347,9 +347,10 @@
 
 
 def make_gate(width, turn):
-    def gate(masked, w_gate, gates, swap, back):
+    def gate(masked, w_gate, w_proj, gain, gates, proj, swap, back):
+        proj[...] = dot_t(masked[...], w_proj[...])
         value = dot(masked[...], w_gate[...])
-        gates[...] = value / (1.0 + jnp.exp(-value))
+        gates[...] = gain[...] * (value / (1.0 + jnp.exp(-value)))
         count = masked.shape[0]
         swap[...] = swap_matrix(count, width)
         back[...] = swap_matrix(count, count // width, turn)
@@ -357,8 +358,8 @@
     return gate
 
 
-def finish(columns, gates, masked, w_out, gain, back, mixed, rows_out, sems):
-    act = (normed(dot(back[...], columns[...]), gain[...]) * gates[...]).astype(bf16)
+def finish(columns, gates, masked, w_out, back, mixed, rows_out, sems):
+    act = normed(dot(back[...], columns[...]), gates[...]).astype(bf16)
     copies = []
     part = mixed.shape[1] // sems.shape[0]
     for k in range(sems.shape[0]):
@@ -427,14 +428,13 @@
         row(step_bias_across),
         row(rates_across),
     )
-    masked, values, proj, b_rows, run_col, less_row, payload = call(
+    masked, values, b_rows, run_row, less_row, payload = call(
         prepare,
         (
             shape((count, width_all), bf16),
             shape((count, width_all), bf16),
-            shape((count, proj_count), f32),
             shape((state_count, count), f32),
-            shape((LANES, blocks * head_count), f32),
+            shape((blocks * head_count, LANES), f32),
             shape((blocks * head_count, LANES), f32),
             shape((state_rows + 2 * line_count, width_all), bf16),
         ),
@@ -460,15 +460,18 @@
     )
     came = shifted(sent, "cols", 2)
     early, _ = lax.optimization_barrier((masked, sent))
-    gates, swap, back = call(
+    gates, proj, swap, back = call(
         make_gate(width, FIRST_DOWN - FIRST_BACK + width),
         (
             shape((count, width_all), f32),
+            shape((count, proj_count), f32),
             shape((count, count), bf16),
             shape((count, count), bf16),
         ),
         early,
         w_gate,
+        w_across.T,
+        row(gain_final),
         flops=5 * 10**8,
         name="gate",
     )
@@ -490,16 +493,16 @@
     came = shifted(sent, "cols", 4)
     values, _ = lax.optimization_barrier((values, sent))
     passed = tuple(
-        row(x) for x in (step_bias_down, rates_down, skip_down, gain_across, gain_final)
-    )
-    outputs, reach, bias_down, rate_down, skips_down, gains_across, gains_final = call(
+        row(x) for x in (step_bias_down, rates_down, skip_down, gain_across)
+    )
+    outputs, reach, bias_down, rate_down, skips_down, gains_across = call(
         make_within(width),
         (shape((count, width_all), f32), shape((count, width_all), f32))
         + tuple(shape(x.shape, x.dtype) for x in passed),
         values,
         proj,
         b_rows,
-        run_col,
+        run_row,
         less_row,
         row(skip_across),
         *passed,
@@ -546,7 +549,6 @@
         gates,
         masked,
         w_out,
-        gains_final,
         back,
         flops=5 * 10**8,
         name="finish",

time: 79.1 us -> 79 us (level)
  no operation moved by 1% of the time
where the time goes in v4:
time: 79 us; the launch traced here: 78.6 us
  blocking collectives  49 us (62%)
  waiting for transfers between devices  12.2 us (15%)
  Pallas kernels  10.2 us (13%)
  starting transfers between devices  6.31 us (8%)
    all_to_all x2, blocking collectives, on_device(): lax.all_to_all(x.reshape(split), 'rows', 0, 0, axis_index_groups=order(fi...  49 us
    ppermute x3, waiting for transfers between devices, shifted(): return lax.ppermute(value, axis, [(i, i + by) for i in range(count - by)])  12.2 us
    pallas_call x8, Pallas kernels, call(): pl.pallas_call(body, out_shape=out_shape, in_specs=[ins] * len(args), out...  10.2 us
    ppermute x3, starting transfers between devices, shifted(): return lax.ppermute(value, axis, [(i, i + by) for i in range(count - by)])  6.31 us
  transfers between devices with their start and end apart: 3, of which 3 were waited for; matrix products, arithmetic and copies ran while one was open for 0% of the time, Pallas kernels for 3%

profile of v4, /device:TPU:4, one launch (start us, length us, event | category | flops | bytes accessed | tf_op | source)
XLA Modules:
  0.0 78.6 jit_solution(17999850750706558285)
XLA Ops:
  0.0 2.5 %prepare.1 = (bf16[512,512]{1,0:T(8,128)(2,1)S(1)}, bf16[512,512]{1,0:T(8,128)(2,1)S(1)}, f32[16,512]{1,0:T(8,128)S(1)}, f32[32,128]{1,0:T(8,128)S(1)}, f32[32,1...) custom-call(bf16[512,512]{1,0:T(8,128)(2,1)} %bitcast.29, s32[8,64]{1,0:T(8,128)} %refs_1_.1, bf16[512,512]{1,0:T(8,128)(2,1)} %refs_2_.1, ...), custom_call_target="tpu_custom_call" | custom-call | flops 500000000 | bytes 4194304 | tf_op jit(solution)/shard_map/prepare/pallas_call | solution.py:385
  2.5 0.0 copy-start.2
  2.5 1.9 %collective-permute-start = (bf16[144,512]{1,0:T(8,128)(2,1)S(1)}, bf16[144,512]{1,0:T(8,128)(2,1)S(1)}, u32[]{:S(2)}, u32[]{:S(2)}) collective-permute-start(bf16[144,512]{1,0:T(8,128)(2,1)S(1)} %get-tuple-element.32.own), channel_id=1, source_target_pairs={{0,1},{1,2},{2,3},{3,4},{4,5},{5,6},{6,7},{8,9},{9,10},{10,11},{11... | collective-permute-start | bytes 442376 | tf_op jit(solution)/shard_map/ppermute | solution.py:376
  4.5 4.5 %collective-permute-done.came = bf16[144,512]{1,0:T(8,128)(2,1)S(1)} collective-permute-done((bf16[144,512]{1,0:T(8,128)(2,1)S(1)}, bf16[144,512]{1,0:T(8,128)(2,1)S(1)}, u32[]{:S(2)}, u32[]{:S(2)}) %collective-permute-start) | collective-permute-done | bytes 147488 | tf_op jit(solution)/shard_map/ppermute | solution.py:376
  9.0 0.1 first_step.1
  9.1 0.0 copy-start.4
  9.1 3.1 %collective-permute-start.1 = (bf16[144,512]{1,0:T(8,128)(2,1)S(1)}, bf16[144,512]{1,0:T(8,128)(2,1)S(1)}, u32[]{:S(2)}, u32[]{:S(2)}) collective-permute-start(bf16[144,512]{1,0:T(8,128)(2,1)S(1)} %get-tuple-element.33), channel_id=1, source_target_pairs={{0,2},{1,3},{2,4},{3,5},{4,6},{5,7},{8,10},{9,11},{10,12},{11,13},... | collective-permute-start | bytes 442376 | tf_op jit(solution)/shard_map/ppermute | solution.py:376
  12.2 1.2 %gate.1 = (f32[512,512]{1,0:T(8,128)S(1)}, f32[512,40]{1,0:T(8,128)S(1)}, bf16[512,512]{1,0:T(8,128)(2,1)S(1)}, bf16[512,512]{1,0:T(8,128)(2,1)S(1)}) custom-call(bf16[512,512]{1,0:T(8,128)(2,1)S(1)} %get-tuple-element.35.masked, bf16[512,512]{1,0:T(8,128)(2,1)S(1)} %copy-done.1, bf16[40,512]{1,0:T(8,128)(2,1)S(1)} %bitcast.21, f32[1,512]{1,0:T(1,128)S(1)} %bitcast.23), custom_call_target="tpu_custom_call" | custom-call | flops 500000000 | bytes 4194304 | tf_op jit(solution)/shard_map/gate/pallas_call | solution.py:385
  13.4 2.7 %collective-permute-done.1.came = bf16[144,512]{1,0:T(8,128)(2,1)S(1)} collective-permute-done((bf16[144,512]{1,0:T(8,128)(2,1)S(1)}, bf16[144,512]{1,0:T(8,128)(2,1)S(1)}, u32[]{:S(2)}, u32[]{:S(2)}) %collective-permute-start.1) | collective-permute-done | bytes 147488 | tf_op jit(solution)/shard_map/ppermute | solution.py:376
  16.1 0.1 second_step.1
  16.2 1.3 %collective-permute-start.2 = (bf16[128,512]{1,0:T(8,128)(2,1)S(1)}, bf16[128,512]{1,0:T(8,128)(2,1)S(1)}, u32[]{:S(2)}, u32[]{:S(2)}) collective-permute-start(bf16[128,512]{1,0:T(8,128)(2,1)S(1)} %get-tuple-element.40), channel_id=1, source_target_pairs={{0,4},{1,5},{2,6},{3,7},{8,12},{9,13},{10,14},{11,15},{16,20},{17,... | collective-permute-start | bytes 393224 | tf_op jit(solution)/shard_map/ppermute | solution.py:376
  17.5 0.0 copy-start.5
  17.5 0.0 copy-start.6
  17.5 0.0 copy-start.8
  17.5 0.6 copy-done.5
  18.2 0.0 copy-done.8
  18.2 1.4 %within_rows.1 = (f32[512,512]{1,0:T(8,128)S(1)}, f32[512,512]{1,0:T(8,128)S(1)}, f32[1,8]{1,0:T(1,128)S(1)}, f32[1,8]{1,0:T(1,128)S(1)}, f32[1,8]{1,0:T(1,128)S(1)}, /*index=5*/f32[1,512]{1,0:T(1,128)S(1)}) custom-call(bf16[512,512]{1,0:T(8,128)(2,1)S(1)} %get-tuple-element.41.values, f32[512,40]{1,0:T(8,128)S(1)} %get-tuple-element.42.proj, ...), custom_call_target="tpu_custom_call" | custom-call | flops 1000000000 | bytes 4194304 | tf_op jit(solution)/shard_map/within_rows/pallas_call | solution.py:385
  19.6 5.0 %collective-permute-done.2.came = bf16[128,512]{1,0:T(8,128)(2,1)S(1)} collective-permute-done((bf16[128,512]{1,0:T(8,128)(2,1)S(1)}, bf16[128,512]{1,0:T(8,128)(2,1)S(1)}, u32[]{:S(2)}, u32[]{:S(2)}) %collective-permute-start.2) | collective-permute-done | bytes 131104 | tf_op jit(solution)/shard_map/ppermute | solution.py:376
  24.6 1.0 %finish_rows.1 = bf16[512,512]{1,0:T(8,128)(2,1)S(1)} custom-call(f32[512,512]{1,0:T(8,128)S(1)} %get-tuple-element.46.outputs, f32[512,512]{1,0:T(8,128)S(1)} %get-tuple-element.47.reach, f32[512,40]{1,0:T(8,128)S(1)} %get-tuple-element.42.proj, f32[128,512]{1,0:T(8,128)S(1)} %get-tuple-element.48.states, f32[8,512]{1,0:T(8,128)S(1)} %get-tuple-element.49.spans, ...), custom_call_target="tpu_custom_call" | custom-call | flops 500000000 | bytes 4194304 | tf_op jit(solution)/shard_map/finish_rows/pallas_call | solution.py:385
  25.5 0.0 copy-start.3
  25.5 28.3 %all_to_all.10 = bf16[64,8,512]{2,1,0:T(8,128)(2,1)S(1)} all-to-all(bf16[64,8,512]{2,1,0:T(8,128)(2,1)S(1)} %bitcast.16), channel_id=1, replica_groups={{368,376,384,392,400,408,416,424,432,440,448,456,464,472,480,488,496,50..., dimensions={0} | all-to-all | bytes 1048576 | tf_op jit(solution)/shard_map/all_to_all | solution.py:529
  53.8 2.4 %scan_columns.1 = bf16[512,512]{1,0:T(8,128)(2,1)S(1)} custom-call(bf16[512,512]{1,0:T(8,128)(2,1)S(1)} %bitcast.18, bf16[40,512]{1,0:T(8,128)(2,1)S(1)} %bitcast.22, f32[1,8]{1,0:T(1,128)S(1)} %get-tuple-element.52.bias, f32[1,8]{1,0:T(1,128)S(1)} %get-tuple-element.53.rates, f32[1,8]{1,0:T(1,128)S(1)} %get-tuple-element.54.skips), custom_call_target="tpu_custom_call" | custom-call | flops 1000000000 | bytes 4194304 | tf_op jit(solution)/shard_map/scan_columns/pallas_call | solution.py:385
  56.2 20.7 %all_to_all.11 = bf16[64,8,512]{2,1,0:T(8,128)(2,1)S(1)} all-to-all(bf16[64,8,512]{2,1,0:T(8,128)(2,1)S(1)} %bitcast.19), channel_id=1, replica_groups={{368,376,384,392,400,408,416,424,432,440,448,456,464,472,480,488,496,50..., dimensions={0} | all-to-all | bytes 1048576 | tf_op jit(solution)/shard_map/all_to_all | solution.py:529
  76.9 1.6 %finish.1 = bf16[512,512]{1,0:T(8,128)(2,1)} custom-call(bf16[512,512]{1,0:T(8,128)(2,1)S(1)} %bitcast.17, f32[512,512]{1,0:T(8,128)S(1)} %get-tuple-element.55.gates, bf16[512,512]{1,0:T(8,128)(2,1)S(1)} %get-tuple-element.35.masked, bf16[512,512]{1,0:T(8,128)(2,1)S(1)} %copy-done, bf16[512,512]{1,0:T(8,128)(2,1)S(1)} %get-tuple-element.56.back), custom_call_target="tpu_custom_call" | custom-call | flops 500000000 | bytes 4194304 | tf_op jit(solution)/shard_map/finish/pallas_call | solution.py:385
  (12 shorter events, 0.0 us)
Async XLA Ops:
  0.0 12.2 %copy-start.1 = (bf16[512,512]{1,0:T(8,128)(2,1)S(1)}, bf16[512,512]{1,0:T(8,128)(2,1)}, u32[]{:S(2)}) copy-start(bf16[512,512]{1,0:T(8,128)(2,1)} %w_gate.1) | copy-start | bytes 1572868
  2.5 9.7 %copy-start.2 = (bf16[512,40]{0,1:T(8,128)(2,1)S(1)}, bf16[512,40]{0,1:T(8,128)(2,1)}, u32[]{:S(2)}) copy-start(bf16[512,40]{0,1:T(8,128)(2,1)} %param.18) | copy-start | bytes 122884
  2.5 6.5 %collective-permute-start = (bf16[144,512]{1,0:T(8,128)(2,1)S(1)}, bf16[144,512]{1,0:T(8,128)(2,1)S(1)}, u32[]{:S(2)}, u32[]{:S(2)}) collective-permute-start(bf16[144,512]{1,0:T(8,128)(2,1)S(1)} %get-tuple-element.32.own), channel_id=1, source_target_pairs={{0,1},{1,2},{2,3},{3,4},{4,5},{5,6},{6,7},{8,9},{9,10},{10,11},{11... | collective-permute-start | bytes 442376 | tf_op jit(solution)/shard_map/ppermute | solution.py:376
  9.1 3.1 %copy-start.4 = (f32[512]{0:T(512)S(1)}, f32[512]{0:T(512)}, u32[]{:S(2)}) copy-start(f32[512]{0:T(512)} %param.29) | copy-start | bytes 6148
  9.1 7.0 %collective-permute-start.1 = (bf16[144,512]{1,0:T(8,128)(2,1)S(1)}, bf16[144,512]{1,0:T(8,128)(2,1)S(1)}, u32[]{:S(2)}, u32[]{:S(2)}) collective-permute-start(bf16[144,512]{1,0:T(8,128)(2,1)S(1)} %get-tuple-element.33), channel_id=1, source_target_pairs={{0,2},{1,3},{2,4},{3,5},{4,6},{5,7},{8,10},{9,11},{10,12},{11,13},... | collective-permute-start | bytes 442376 | tf_op jit(solution)/shard_map/ppermute | solution.py:376
  16.1 1.4 %copy-start.9 = (f32[8]{0:T(128)S(1)}, f32[8]{0:T(128)}, u32[]{:S(2)}) copy-start(f32[8]{0:T(128)} %param.27) | copy-start | bytes 100
  16.2 8.4 %collective-permute-start.2 = (bf16[128,512]{1,0:T(8,128)(2,1)S(1)}, bf16[128,512]{1,0:T(8,128)(2,1)S(1)}, u32[]{:S(2)}, u32[]{:S(2)}) collective-permute-start(bf16[128,512]{1,0:T(8,128)(2,1)S(1)} %get-tuple-element.40), channel_id=1, source_target_pairs={{0,4},{1,5},{2,6},{3,7},{8,12},{9,13},{10,14},{11,15},{16,20},{17,... | collective-permute-start | bytes 393224 | tf_op jit(solution)/shard_map/ppermute | solution.py:376
  17.5 0.7 copy-start.5
  17.5 0.7 copy-start.6
  17.5 0.7 copy-start.7
  17.5 0.7 copy-start.8
  25.5 28.3 %copy-start.3 = (bf16[512,40]{0,1:T(8,128)(2,1)S(1)}, bf16[512,40]{0,1:T(8,128)(2,1)}, u32[]{:S(2)}) copy-start(bf16[512,40]{0,1:T(8,128)(2,1)} %param.19) | copy-start | bytes 122884
  56.2 20.7 %copy-start = (bf16[512,512]{1,0:T(8,128)(2,1)S(1)}, bf16[512,512]{1,0:T(8,128)(2,1)}, u32[]{:S(2)}) copy-start(bf16[512,512]{1,0:T(8,128)(2,1)} %w_out.1) | copy-start | bytes 1572868

commit v5 on v4

--- a/solution.py
+++ b/solution.py
@@ -201,14 +201,17 @@
 def first_step(own, came, state, span, sent):
     line_count = span.shape[0]
     state_count = state.shape[0] // line_count
-    decays, before = read_decays(own, line_count), read_decays(came, line_count)
-    span[...] = before
-    keep_decays(sent, decays * before)
+    later = lax.rem(lax.axis_index("cols"), 2) == 1
+    mine, other = read_decays(own, line_count), read_decays(came, line_count)
+    span[...] = jnp.where(later, other, 1.0)
+    keep_decays(sent, mine * other)
+    second = jnp.where(later, mine, other)
     for r in range(line_count):
         at = line_rows(r, state_count)
-        entered = came[at, :].astype(f32)
-        state[at, :] = entered
-        sent[at, :] = (own[at, :].astype(f32) + decays[r : r + 1] * entered).astype(bf16)
+        here, there = own[at, :].astype(f32), came[at, :].astype(f32)
+        state[at, :] = jnp.where(later, there, 0.0)
+        head, tail = jnp.where(later, there, here), jnp.where(later, here, there)
+        sent[at, :] = (tail + second[r : r + 1] * head).astype(bf16)
 
 
 def second_step(own, came, state, span, states, spans, sent):
@@ -219,8 +222,8 @@
     spans[...] = over * before
     for r in range(line_count):
         at = line_rows(r, state_count)
-        entered = state[at, :] + over[r : r + 1] * came[at, :].astype(f32)
-        states[at, :] = entered
+        entered = came[at, :].astype(f32)
+        states[at, :] = state[at, :] + over[r : r + 1] * entered
         sent[at, :] = (own[at, :].astype(f32) + decays[r : r + 1] * entered).astype(bf16)
 
 
@@ -380,7 +383,18 @@
 IN_PLACE = pl.BlockSpec(memory_space=pltpu.HBM)
 
 
-def call(body, out_shape, *args, flops=0, name=None, ins=IN_VMEM, outs=IN_VMEM, scratch=()):
+def on_core(core, body, skipped=0):
+    def guarded(*refs):
+        @pl.when(lax.rem(lax.axis_index("cols"), 2) == core)
+        def _():
+            body(*refs[skipped:])
+
+    return guarded
+
+
+def call(
+    body, out_shape, *args, flops=0, name=None, ins=IN_VMEM, outs=IN_VMEM, scratch=(), aliases={}
+):
     single = not isinstance(out_shape, tuple)
     return pl.pallas_call(
         body,
@@ -389,6 +403,7 @@
         out_specs=outs if single else tuple(outs for _ in out_shape),
         scratch_shapes=scratch,
         name=name,
+        input_output_aliases=aliases,
         cost_estimate=pl.CostEstimate(flops=flops, bytes_accessed=4 << 20, transcendentals=0),
         compiler_params=pltpu.CompilerParams(vmem_limit_bytes=24 << 20),
     )(*args)
@@ -445,7 +460,8 @@
         scratch=[pltpu.VMEM(x.shape, x.dtype) for x in given]
         + [pltpu.SemaphoreType.DMA((len(given),))],
     )
-    came = shifted(payload, "cols", 1)
+    count_of = lax.axis_size("cols")
+    came = lax.ppermute(payload, "cols", [(i, i ^ 1) for i in range(count_of)])
     state, span, sent = call(
         first_step,
         (
@@ -458,22 +474,28 @@
         flops=10**6,
         name="first_step",
     )
+    gate_shapes = (
+        shape((count, width_all), f32),
+        shape((count, proj_count), f32),
+        shape((count, count), bf16),
+        shape((count, count), bf16),
+    )
+    gate = make_gate(width, FIRST_DOWN - FIRST_BACK + width)
+    early, _ = lax.optimization_barrier((masked, sent))
+    gate_args = (early, w_gate, w_across.T, row(gain_final))
+    half_made = call(
+        on_core(0, gate), gate_shapes, *gate_args, flops=5 * 10**8, name="gate_first"
+    )
+    sent, half_made = lax.optimization_barrier((sent, half_made))
     came = shifted(sent, "cols", 2)
-    early, _ = lax.optimization_barrier((masked, sent))
     gates, proj, swap, back = call(
-        make_gate(width, FIRST_DOWN - FIRST_BACK + width),
-        (
-            shape((count, width_all), f32),
-            shape((count, proj_count), f32),
-            shape((count, count), bf16),
-            shape((count, count), bf16),
-        ),
-        early,
-        w_gate,
-        w_across.T,
-        row(gain_final),
+        on_core(1, gate, 4),
+        gate_shapes,
+        *half_made,
+        *gate_args,
         flops=5 * 10**8,
-        name="gate",
+        name="gate_second",
+        aliases={i: i for i in range(4)},
     )
     came, gates = lax.optimization_barrier((came, gates))
     states, spans, sent = call(
@@ -483,7 +505,7 @@
             shape((line_count, width_all), f32),
             shape((state_rows, width_all), bf16),
         ),
-        payload,
+        sent,
         came,
         state,
         span,

time: 79 us -> 77.9 us (0.986)
  waiting for transfers between devices: 12.2 us -> 10.2 us
    ppermute x3 -> x2, waiting for transfers between devices: 12.2 us -> 8.88 us  [shifted(): return lax.ppermute(value, axis, [(i, i + by) for i in range(count - by)])]
    ppermute x3 -> x2, starting transfers between devices: 6.31 us -> 4.39 us  [shifted(): return lax.ppermute(value, axis, [(i, i + by) for i in range(count - by)])]
    ppermute x0 -> x1, starting transfers between devices: none -> 1.92 us  [on_device(): came = lax.ppermute(payload, 'cols', [(i, i ^ 1) for i in range(count_of)])]
    ppermute x0 -> x1, waiting for transfers between devices: none -> 1.34 us  [on_device(): came = lax.ppermute(payload, 'cols', [(i, i ^ 1) for i in range(count_of)])]
    pallas_call x8 -> x9, Pallas kernels: 10.2 us -> 10.3 us  [call(): pl.pallas_call(body, out_shape=out_shape, in_specs=[ins] * len(args), out...]
  transfers between devices with their start and end apart: 3 -> 3, of which waited for: 3 -> 3; matrix products, arithmetic and copies ran while one was open for 0% -> 0% of each run, Pallas kernels for 3% -> 2%
where the time goes in v5:
time: 77.9 us; the launch traced here: 77.5 us
  blocking collectives  49.2 us (63%)
  Pallas kernels  10.3 us (13%)
  waiting for transfers between devices  10.2 us (13%)
  starting transfers between devices  6.31 us (8%)
  local copies, waits for them, and re-layouts  1.35 us (2%)
    all_to_all x2, blocking collectives, on_device(): lax.all_to_all(x.reshape(split), 'rows', 0, 0, axis_index_groups=order(fi...  49.2 us
    pallas_call x9, Pallas kernels, call(): pl.pallas_call(body, out_shape=out_shape, in_specs=[ins] * len(args), out...  10.3 us
    ppermute x2, waiting for transfers between devices, shifted(): return lax.ppermute(value, axis, [(i, i + by) for i in range(count - by)])  8.88 us
    ppermute x2, starting transfers between devices, shifted(): return lax.ppermute(value, axis, [(i, i + by) for i in range(count - by)])  4.39 us
    ppermute x1, starting transfers between devices, on_device(): came = lax.ppermute(payload, 'cols', [(i, i ^ 1) for i in range(count_of)])  1.92 us
  transfers between devices with their start and end apart: 3, of which 3 were waited for; matrix products, arithmetic and copies ran while one was open for 0% of the time, Pallas kernels for 2%

profile of v5, /device:TPU:4, one launch (start us, length us, event | category | flops | bytes accessed | tf_op | source)
XLA Modules:
  0.0 77.5 jit_solution(1510154103084330853)
XLA Ops:
  0.0 2.5 %prepare.1 = (bf16[512,512]{1,0:T(8,128)(2,1)S(1)}, bf16[512,512]{1,0:T(8,128)(2,1)S(1)}, f32[16,512]{1,0:T(8,128)S(1)}, f32[32,128]{1,0:T(8,128)S(1)}, f32[32,1...) custom-call(bf16[512,512]{1,0:T(8,128)(2,1)} %bitcast.31, s32[8,64]{1,0:T(8,128)} %refs_1_.2, bf16[512,512]{1,0:T(8,128)(2,1)} %refs_2_.1, ...), custom_call_target="tpu_custom_call" | custom-call | flops 500000000 | bytes 4194304 | tf_op jit(solution)/shard_map/prepare/pallas_call | solution.py:399
  2.5 0.0 copy-start.2
  2.5 1.9 %collective-permute-start = (bf16[144,512]{1,0:T(8,128)(2,1)S(1)}, bf16[144,512]{1,0:T(8,128)(2,1)S(1)}, u32[]{:S(2)}, u32[]{:S(2)}) collective-permute-start(bf16[144,512]{1,0:T(8,128)(2,1)S(1)} %get-tuple-element.41.own), channel_id=1, source_target_pairs={{0,1},{1,0},{2,3},{3,2},{4,5},{5,4},{6,7},{7,6},{8,9},{9,8},{10,11... | collective-permute-start | bytes 442376 | tf_op jit(solution)/shard_map/ppermute | solution.py:464
  4.5 1.3 %collective-permute-done.came = bf16[144,512]{1,0:T(8,128)(2,1)S(1)} collective-permute-done((bf16[144,512]{1,0:T(8,128)(2,1)S(1)}, bf16[144,512]{1,0:T(8,128)(2,1)S(1)}, u32[]{:S(2)}, u32[]{:S(2)}) %collective-permute-start) | collective-permute-done | bytes 147488 | tf_op jit(solution)/shard_map/ppermute | solution.py:464
  5.8 0.1 first_step.1
  5.9 0.0 copy-start.3
  5.9 0.7 copy-done.3
  6.6 1.2 %gate_first.1 = (f32[512,512]{1,0:T(8,128)S(1)}, f32[512,40]{1,0:T(8,128)S(1)}, bf16[512,512]{1,0:T(8,128)(2,1)S(1)}, bf16[512,512]{1,0:T(8,128)(2,1)S(1)}) custom-call(bf16[512,512]{1,0:T(8,128)(2,1)S(1)} %get-tuple-element.44.refs_0_.refs_4_.masked, bf16[512,512]{1,0:T(8,128)(2,1)S(1)} %copy-done.1, bf16[40,512]{1,0:T(8,128)(2,1)S(1)} %bitcast.21, ...), custom_call_target="tpu_custom_call" | custom-call | flops 500000000 | bytes 4194304 | tf_op jit(solution)/shard_map/gate_first/pallas_call | solution.py:399
  7.8 3.1 %collective-permute-start.1 = (bf16[144,512]{1,0:T(8,128)(2,1)S(1)}, bf16[144,512]{1,0:T(8,128)(2,1)S(1)}, u32[]{:S(2)}, u32[]{:S(2)}) collective-permute-start(bf16[144,512]{1,0:T(8,128)(2,1)S(1)} %get-tuple-element.49.own), channel_id=1, source_target_pairs={{0,2},{1,3},{2,4},{3,5},{4,6},{5,7},{8,10},{9,11},{10,12},{11,13},... | collective-permute-start | bytes 442376 | tf_op jit(solution)/shard_map/ppermute | solution.py:379
  10.9 3.9 %collective-permute-done.1.came = bf16[144,512]{1,0:T(8,128)(2,1)S(1)} collective-permute-done((bf16[144,512]{1,0:T(8,128)(2,1)S(1)}, bf16[144,512]{1,0:T(8,128)(2,1)S(1)}, u32[]{:S(2)}, u32[]{:S(2)}) %collective-permute-start.1) | collective-permute-done | bytes 147488 | tf_op jit(solution)/shard_map/ppermute | solution.py:379
  14.8 0.1 second_step.1
  14.9 1.3 %collective-permute-start.2 = (bf16[128,512]{1,0:T(8,128)(2,1)S(1)}, bf16[128,512]{1,0:T(8,128)(2,1)S(1)}, u32[]{:S(2)}, u32[]{:S(2)}) collective-permute-start(bf16[128,512]{1,0:T(8,128)(2,1)S(1)} %get-tuple-element.58), channel_id=1, source_target_pairs={{0,4},{1,5},{2,6},{3,7},{8,12},{9,13},{10,14},{11,15},{16,20},{17,... | collective-permute-start | bytes 393224 | tf_op jit(solution)/shard_map/ppermute | solution.py:379
  16.2 0.0 copy-start.6
  16.2 0.0 copy-start.7
  16.3 0.6 copy-done.5
  16.9 0.0 copy-done.8
  16.9 1.4 %within_rows.1 = (f32[512,512]{1,0:T(8,128)S(1)}, f32[512,512]{1,0:T(8,128)S(1)}, f32[1,8]{1,0:T(1,128)S(1)}, f32[1,8]{1,0:T(1,128)S(1)}, f32[1,8]{1,0:T(1,128)S(1)}, /*index=5*/f32[1,512]{1,0:T(1,128)S(1)}) custom-call(bf16[512,512]{1,0:T(8,128)(2,1)S(1)} %get-tuple-element.59.values, f32[512,40]{1,0:T(8,128)S(1)} %get-tuple-element.60.proj, ...), custom_call_target="tpu_custom_call" | custom-call | flops 1000000000 | bytes 4194304 | tf_op jit(solution)/shard_map/within_rows/pallas_call | solution.py:399
  18.3 5.0 %collective-permute-done.2.came = bf16[128,512]{1,0:T(8,128)(2,1)S(1)} collective-permute-done((bf16[128,512]{1,0:T(8,128)(2,1)S(1)}, bf16[128,512]{1,0:T(8,128)(2,1)S(1)}, u32[]{:S(2)}, u32[]{:S(2)}) %collective-permute-start.2) | collective-permute-done | bytes 131104 | tf_op jit(solution)/shard_map/ppermute | solution.py:379
  23.3 1.0 %finish_rows.1 = bf16[512,512]{1,0:T(8,128)(2,1)S(1)} custom-call(f32[512,512]{1,0:T(8,128)S(1)} %get-tuple-element.64.outputs, f32[512,512]{1,0:T(8,128)S(1)} %get-tuple-element.65.reach, f32[512,40]{1,0:T(8,128)S(1)} %get-tuple-element.60.proj, f32[128,512]{1,0:T(8,128)S(1)} %get-tuple-element.66.states, f32[8,512]{1,0:T(8,128)S(1)} %get-tuple-element.67.spans, ...), custom_call_target="tpu_custom_call" | custom-call | flops 500000000 | bytes 4194304 | tf_op jit(solution)/shard_map/finish_rows/pallas_call | solution.py:399
  24.2 28.4 %all_to_all.10 = bf16[64,8,512]{2,1,0:T(8,128)(2,1)S(1)} all-to-all(bf16[64,8,512]{2,1,0:T(8,128)(2,1)S(1)} %bitcast.16), channel_id=1, replica_groups={{368,376,384,392,400,408,416,424,432,440,448,456,464,472,480,488,496,50..., dimensions={0} | all-to-all | bytes 1048576 | tf_op jit(solution)/shard_map/all_to_all | solution.py:551
  52.6 2.4 %scan_columns.1 = bf16[512,512]{1,0:T(8,128)(2,1)S(1)} custom-call(bf16[512,512]{1,0:T(8,128)(2,1)S(1)} %bitcast.18, bf16[40,512]{1,0:T(8,128)(2,1)S(1)} %bitcast.25, f32[1,8]{1,0:T(1,128)S(1)} %get-tuple-element.70.bias, f32[1,8]{1,0:T(1,128)S(1)} %get-tuple-element.71.rates, f32[1,8]{1,0:T(1,128)S(1)} %get-tuple-element.72.skips), custom_call_target="tpu_custom_call" | custom-call | flops 1000000000 | bytes 4194304 | tf_op jit(solution)/shard_map/scan_columns/pallas_call | solution.py:399
  55.0 0.0 copy-start
  55.0 20.9 %all_to_all.11 = bf16[64,8,512]{2,1,0:T(8,128)(2,1)S(1)} all-to-all(bf16[64,8,512]{2,1,0:T(8,128)(2,1)S(1)} %bitcast.19), channel_id=1, replica_groups={{368,376,384,392,400,408,416,424,432,440,448,456,464,472,480,488,496,50..., dimensions={0} | all-to-all | bytes 1048576 | tf_op jit(solution)/shard_map/all_to_all | solution.py:551
  75.9 1.6 %finish.1 = bf16[512,512]{1,0:T(8,128)(2,1)} custom-call(bf16[512,512]{1,0:T(8,128)(2,1)S(1)} %bitcast.17, f32[512,512]{1,0:T(8,128)S(1)} %get-tuple-element.73.gates, bf16[512,512]{1,0:T(8,128)(2,1)S(1)} %get-tuple-element.44.refs_0_.refs_4_.masked, bf16[512,512]{1,0:T(8,128)(2,1)S(1)} %copy-done, bf16[512,512]{1,0:T(8,128)(2,1)S(1)} %get-tuple-element.74.back), custom_call_target="tpu_custom_call" | custom-call | flops 500000000 | bytes 4194304 | tf_op jit(solution)/shard_map/finish/pallas_call | solution.py:399
  (13 shorter events, 0.0 us)
Async XLA Ops:
  0.0 5.9 %copy-start.1 = (bf16[512,512]{1,0:T(8,128)(2,1)S(1)}, bf16[512,512]{1,0:T(8,128)(2,1)}, u32[]{:S(2)}) copy-start(bf16[512,512]{1,0:T(8,128)(2,1)} %refs_5_.1) | copy-start | bytes 1572868
  2.5 3.4 %copy-start.2 = (bf16[512,40]{0,1:T(8,128)(2,1)S(1)}, bf16[512,40]{0,1:T(8,128)(2,1)}, u32[]{:S(2)}) copy-start(bf16[512,40]{0,1:T(8,128)(2,1)} %param.18) | copy-start | bytes 122884
  2.5 3.3 %collective-permute-start = (bf16[144,512]{1,0:T(8,128)(2,1)S(1)}, bf16[144,512]{1,0:T(8,128)(2,1)S(1)}, u32[]{:S(2)}, u32[]{:S(2)}) collective-permute-start(bf16[144,512]{1,0:T(8,128)(2,1)S(1)} %get-tuple-element.41.own), channel_id=1, source_target_pairs={{0,1},{1,0},{2,3},{3,2},{4,5},{5,4},{6,7},{7,6},{8,9},{9,8},{10,11... | collective-permute-start | bytes 442376 | tf_op jit(solution)/shard_map/ppermute | solution.py:464
  5.9 0.7 copy-start.3
  7.8 7.0 %collective-permute-start.1 = (bf16[144,512]{1,0:T(8,128)(2,1)S(1)}, bf16[144,512]{1,0:T(8,128)(2,1)S(1)}, u32[]{:S(2)}, u32[]{:S(2)}) collective-permute-start(bf16[144,512]{1,0:T(8,128)(2,1)S(1)} %get-tuple-element.49.own), channel_id=1, source_target_pairs={{0,2},{1,3},{2,4},{3,5},{4,6},{5,7},{8,10},{9,11},{10,12},{11,13},... | collective-permute-start | bytes 442376 | tf_op jit(solution)/shard_map/ppermute | solution.py:379
  14.8 1.4 %copy-start.9 = (f32[8]{0:T(128)S(1)}, f32[8]{0:T(128)}, u32[]{:S(2)}) copy-start(f32[8]{0:T(128)} %param.27) | copy-start | bytes 100
  14.9 8.4 %collective-permute-start.2 = (bf16[128,512]{1,0:T(8,128)(2,1)S(1)}, bf16[128,512]{1,0:T(8,128)(2,1)S(1)}, u32[]{:S(2)}, u32[]{:S(2)}) collective-permute-start(bf16[128,512]{1,0:T(8,128)(2,1)S(1)} %get-tuple-element.58), channel_id=1, source_target_pairs={{0,4},{1,5},{2,6},{3,7},{8,12},{9,13},{10,14},{11,15},{16,20},{17,... | collective-permute-start | bytes 393224 | tf_op jit(solution)/shard_map/ppermute | solution.py:379
  16.2 0.7 copy-start.5
  16.2 0.7 copy-start.6
  16.2 0.7 copy-start.7
  16.2 0.7 copy-start.8
  24.2 28.4 %copy-start.4 = (bf16[512,40]{0,1:T(8,128)(2,1)S(1)}, bf16[512,40]{0,1:T(8,128)(2,1)}, u32[]{:S(2)}) copy-start(bf16[512,40]{0,1:T(8,128)(2,1)} %param.19) | copy-start | bytes 122884
  55.0 20.9 %copy-start = (bf16[512,512]{1,0:T(8,128)(2,1)S(1)}, bf16[512,512]{1,0:T(8,128)(2,1)}, u32[]{:S(2)}) copy-start(bf16[512,512]{1,0:T(8,128)(2,1)} %w_out.1) | copy-start | bytes 1572868

commit v6 on v5

--- a/solution.py
+++ b/solution.py
@@ -10,6 +10,7 @@
 bf16, f32 = jnp.bfloat16, jnp.float32
 LANES = 128
 CAP = 80.0
+LOG2E = 1.4426950408889634
 FIRST_DOWN = 46
 FIRST_BACK = 46
 
@@ -64,8 +65,8 @@
 def step_terms(proj_rows, bias, rates, group):
     head_count = bias.shape[-1]
     steps = softplus(proj_rows[-head_count:] + as_column(bias))
-    falls = -steps * as_column(rates)
-    logs = jnp.log(steps)
+    falls = -steps * as_column(rates * LOG2E)
+    logs = jnp.log(steps) * LOG2E
     blocks = proj_rows.shape[1] // LANES
     stack = lambda x: jnp.concatenate([x[:, k * LANES : (k + 1) * LANES] for k in range(blocks)], axis=0)
     falls, logs = stack(falls), stack(logs)
@@ -96,7 +97,7 @@
         for head in (2 * pair, 2 * pair + 1):
             at = block * head_count + head
             spans = run_col[:, at : at + 1] - less_row[at : at + 1, :]
-            weights.append((jnp.exp(jnp.minimum(spans, CAP)) * inter).astype(bf16))
+            weights.append((jnp.exp2(jnp.minimum(spans, CAP)) * inter).astype(bf16))
         both = dot(jnp.concatenate(weights, axis=0), values[:, pair * LANES : (pair + 1) * LANES])
         tiles.append(jnp.where(low_lanes, both[:LANES], both[LANES:]))
     return jnp.concatenate(tiles, axis=1)
@@ -159,7 +160,7 @@
     running, less, totals = step_terms(proj_rows, bias_in[...], rates_in[...], width)
     less_row[...] = less
     run_row[...] = running
-    to_end = jnp.exp(totals - less)
+    to_end = jnp.exp2(totals - less)
     total_cols = jnp.transpose(totals)
     blocks = inputs.shape[0] // LANES
     groups = LANES // width
@@ -170,7 +171,7 @@
         here = (line % groups == g) & (column // head_count == line // groups)
         picked = jnp.where(here, total_cols[g * width : g * width + 1, :], picked)
     lanes = jnp.concatenate([head_lanes(head_count, inputs.shape[1] // head_count)] * blocks, axis=0)
-    decays = jnp.exp(by_ones(picked, lanes.astype(bf16)))
+    decays = jnp.exp2(by_ones(picked, lanes.astype(bf16)))
     keep_decays(payload, decays)
     copies[5].wait()
     narrow = dot(inputs, value_in[...]).astype(bf16)
@@ -257,7 +258,7 @@
     row, lane = iota(shape, 0), iota(shape, 1)
     here = (row // head_count == block) & (row % head_count == lane // (width_all // head_count))
     lanes = jnp.where(here, 1.0, 0.0).astype(bf16)
-    high, low = halves(jnp.exp(run_col_block))
+    high, low = halves(jnp.exp2(run_col_block))
     return dot(high, lanes) + dot(low, lanes)
 
 
@@ -315,7 +316,7 @@
     state_count = (proj.shape[1] - head_count) // 2
     running, less, totals = step_terms(proj_rows, bias[...], rates[...], LANES)
     run_col = jnp.transpose(running)
-    to_end = jnp.exp(totals - less)
+    to_end = jnp.exp2(totals - less)
     total_cols = jnp.transpose(totals)
     lanes = head_lanes(head_count, width_all // head_count)
     skip = spread(skips[...], lanes)
@@ -323,7 +324,7 @@
     shape = (8, blocks * head_count)
     here = iota(shape, 1) // head_count == iota(shape, 0)
     picked = jnp.where(here, jnp.broadcast_to(total_cols[:1], shape), 0.0)
-    decays = jnp.exp(by_ones(picked, jnp.concatenate([lanes] * blocks, axis=0).astype(bf16)))
+    decays = jnp.exp2(by_ones(picked, jnp.concatenate([lanes] * blocks, axis=0).astype(bf16)))
     state = jnp.zeros((state_count, width_all), f32)
     for k in range(blocks):
         at = slice(k * LANES, (k + 1) * LANES)

time: 77.9 us -> 77.9 us (level)
  no operation moved by 1% of the time
where the time goes in v6:
time: 77.9 us; the launch traced here: 77.5 us
  blocking collectives  49.2 us (63%)
  Pallas kernels  10.3 us (13%)
  waiting for transfers between devices  10.2 us (13%)
  starting transfers between devices  6.31 us (8%)
  local copies, waits for them, and re-layouts  1.35 us (2%)
    all_to_all x2, blocking collectives, on_device(): lax.all_to_all(x.reshape(split), 'rows', 0, 0, axis_index_groups=order(fi...  49.2 us
    pallas_call x9, Pallas kernels, call(): pl.pallas_call(body, out_shape=out_shape, in_specs=[ins] * len(args), out...  10.3 us
    ppermute x2, waiting for transfers between devices, shifted(): return lax.ppermute(value, axis, [(i, i + by) for i in range(count - by)])  8.88 us
    ppermute x2, starting transfers between devices, shifted(): return lax.ppermute(value, axis, [(i, i + by) for i in range(count - by)])  4.39 us
    ppermute x1, starting transfers between devices, on_device(): came = lax.ppermute(payload, 'cols', [(i, i ^ 1) for i in range(count_of)])  1.92 us
  transfers between devices with their start and end apart: 3, of which 3 were waited for; matrix products, arithmetic and copies ran while one was open for 0% of the time, Pallas kernels for 2%

profile of v6, /device:TPU:4, one launch (start us, length us, event | category | flops | bytes accessed | tf_op | source)
XLA Modules:
  0.0 77.5 jit_solution(3491381950167451467)
XLA Ops:
  0.0 2.5 %prepare.1 = (bf16[512,512]{1,0:T(8,128)(2,1)S(1)}, bf16[512,512]{1,0:T(8,128)(2,1)S(1)}, f32[16,512]{1,0:T(8,128)S(1)}, f32[32,128]{1,0:T(8,128)S(1)}, f32[32,1...) custom-call(bf16[512,512]{1,0:T(8,128)(2,1)} %bitcast.31, s32[8,64]{1,0:T(8,128)} %refs_1_.2, bf16[512,512]{1,0:T(8,128)(2,1)} %refs_2_.1, ...), custom_call_target="tpu_custom_call" | custom-call | flops 500000000 | bytes 4194304 | tf_op jit(solution)/shard_map/prepare/pallas_call | solution.py:400
  2.5 0.0 copy-start.2
  2.5 1.9 %collective-permute-start = (bf16[144,512]{1,0:T(8,128)(2,1)S(1)}, bf16[144,512]{1,0:T(8,128)(2,1)S(1)}, u32[]{:S(2)}, u32[]{:S(2)}) collective-permute-start(bf16[144,512]{1,0:T(8,128)(2,1)S(1)} %get-tuple-element.41.own), channel_id=1, source_target_pairs={{0,1},{1,0},{2,3},{3,2},{4,5},{5,4},{6,7},{7,6},{8,9},{9,8},{10,11... | collective-permute-start | bytes 442376 | tf_op jit(solution)/shard_map/ppermute | solution.py:465
  4.5 1.3 %collective-permute-done.came = bf16[144,512]{1,0:T(8,128)(2,1)S(1)} collective-permute-done((bf16[144,512]{1,0:T(8,128)(2,1)S(1)}, bf16[144,512]{1,0:T(8,128)(2,1)S(1)}, u32[]{:S(2)}, u32[]{:S(2)}) %collective-permute-start) | collective-permute-done | bytes 147488 | tf_op jit(solution)/shard_map/ppermute | solution.py:465
  5.8 0.1 first_step.1
  5.9 0.7 copy-done.3
  6.6 1.2 %gate_first.1 = (f32[512,512]{1,0:T(8,128)S(1)}, f32[512,40]{1,0:T(8,128)S(1)}, bf16[512,512]{1,0:T(8,128)(2,1)S(1)}, bf16[512,512]{1,0:T(8,128)(2,1)S(1)}) custom-call(bf16[512,512]{1,0:T(8,128)(2,1)S(1)} %get-tuple-element.44.refs_0_.refs_4_.masked, bf16[512,512]{1,0:T(8,128)(2,1)S(1)} %copy-done.1, bf16[40,512]{1,0:T(8,128)(2,1)S(1)} %bitcast.21, ...), custom_call_target="tpu_custom_call" | custom-call | flops 500000000 | bytes 4194304 | tf_op jit(solution)/shard_map/gate_first/pallas_call | solution.py:400
  7.8 3.1 %collective-permute-start.1 = (bf16[144,512]{1,0:T(8,128)(2,1)S(1)}, bf16[144,512]{1,0:T(8,128)(2,1)S(1)}, u32[]{:S(2)}, u32[]{:S(2)}) collective-permute-start(bf16[144,512]{1,0:T(8,128)(2,1)S(1)} %get-tuple-element.49.own), channel_id=1, source_target_pairs={{0,2},{1,3},{2,4},{3,5},{4,6},{5,7},{8,10},{9,11},{10,12},{11,13},... | collective-permute-start | bytes 442376 | tf_op jit(solution)/shard_map/ppermute | solution.py:380
  10.9 3.9 %collective-permute-done.1.came = bf16[144,512]{1,0:T(8,128)(2,1)S(1)} collective-permute-done((bf16[144,512]{1,0:T(8,128)(2,1)S(1)}, bf16[144,512]{1,0:T(8,128)(2,1)S(1)}, u32[]{:S(2)}, u32[]{:S(2)}) %collective-permute-start.1) | collective-permute-done | bytes 147488 | tf_op jit(solution)/shard_map/ppermute | solution.py:380
  14.8 0.1 second_step.1
  14.9 1.3 %collective-permute-start.2 = (bf16[128,512]{1,0:T(8,128)(2,1)S(1)}, bf16[128,512]{1,0:T(8,128)(2,1)S(1)}, u32[]{:S(2)}, u32[]{:S(2)}) collective-permute-start(bf16[128,512]{1,0:T(8,128)(2,1)S(1)} %get-tuple-element.58), channel_id=1, source_target_pairs={{0,4},{1,5},{2,6},{3,7},{8,12},{9,13},{10,14},{11,15},{16,20},{17,... | collective-permute-start | bytes 393224 | tf_op jit(solution)/shard_map/ppermute | solution.py:380
  16.2 0.0 copy-start.5
  16.2 0.0 copy-start.7
  16.2 0.0 copy-start.8
  16.3 0.6 copy-done.5
  16.9 0.0 copy-done.8
  16.9 1.4 %within_rows.1 = (f32[512,512]{1,0:T(8,128)S(1)}, f32[512,512]{1,0:T(8,128)S(1)}, f32[1,8]{1,0:T(1,128)S(1)}, f32[1,8]{1,0:T(1,128)S(1)}, f32[1,8]{1,0:T(1,128)S(1)}, /*index=5*/f32[1,512]{1,0:T(1,128)S(1)}) custom-call(bf16[512,512]{1,0:T(8,128)(2,1)S(1)} %get-tuple-element.59.values, f32[512,40]{1,0:T(8,128)S(1)} %get-tuple-element.60.proj, ...), custom_call_target="tpu_custom_call" | custom-call | flops 1000000000 | bytes 4194304 | tf_op jit(solution)/shard_map/within_rows/pallas_call | solution.py:400
  18.3 5.0 %collective-permute-done.2.came = bf16[128,512]{1,0:T(8,128)(2,1)S(1)} collective-permute-done((bf16[128,512]{1,0:T(8,128)(2,1)S(1)}, bf16[128,512]{1,0:T(8,128)(2,1)S(1)}, u32[]{:S(2)}, u32[]{:S(2)}) %collective-permute-start.2) | collective-permute-done | bytes 131104 | tf_op jit(solution)/shard_map/ppermute | solution.py:380
  23.3 1.0 %finish_rows.1 = bf16[512,512]{1,0:T(8,128)(2,1)S(1)} custom-call(f32[512,512]{1,0:T(8,128)S(1)} %get-tuple-element.64.outputs, f32[512,512]{1,0:T(8,128)S(1)} %get-tuple-element.65.reach, f32[512,40]{1,0:T(8,128)S(1)} %get-tuple-element.60.proj, f32[128,512]{1,0:T(8,128)S(1)} %get-tuple-element.66.states, f32[8,512]{1,0:T(8,128)S(1)} %get-tuple-element.67.spans, ...), custom_call_target="tpu_custom_call" | custom-call | flops 500000000 | bytes 4194304 | tf_op jit(solution)/shard_map/finish_rows/pallas_call | solution.py:400
  24.2 0.0 copy-start.4
  24.2 28.4 %all_to_all.10 = bf16[64,8,512]{2,1,0:T(8,128)(2,1)S(1)} all-to-all(bf16[64,8,512]{2,1,0:T(8,128)(2,1)S(1)} %bitcast.16), channel_id=1, replica_groups={{368,376,384,392,400,408,416,424,432,440,448,456,464,472,480,488,496,50..., dimensions={0} | all-to-all | bytes 1048576 | tf_op jit(solution)/shard_map/all_to_all | solution.py:552
  52.6 2.4 %scan_columns.1 = bf16[512,512]{1,0:T(8,128)(2,1)S(1)} custom-call(bf16[512,512]{1,0:T(8,128)(2,1)S(1)} %bitcast.18, bf16[40,512]{1,0:T(8,128)(2,1)S(1)} %bitcast.25, f32[1,8]{1,0:T(1,128)S(1)} %get-tuple-element.70.bias, f32[1,8]{1,0:T(1,128)S(1)} %get-tuple-element.71.rates, f32[1,8]{1,0:T(1,128)S(1)} %get-tuple-element.72.skips), custom_call_target="tpu_custom_call" | custom-call | flops 1000000000 | bytes 4194304 | tf_op jit(solution)/shard_map/scan_columns/pallas_call | solution.py:400
  55.0 20.9 %all_to_all.11 = bf16[64,8,512]{2,1,0:T(8,128)(2,1)S(1)} all-to-all(bf16[64,8,512]{2,1,0:T(8,128)(2,1)S(1)} %bitcast.19), channel_id=1, replica_groups={{368,376,384,392,400,408,416,424,432,440,448,456,464,472,480,488,496,50..., dimensions={0} | all-to-all | bytes 1048576 | tf_op jit(solution)/shard_map/all_to_all | solution.py:552
  75.9 1.6 %finish.1 = bf16[512,512]{1,0:T(8,128)(2,1)} custom-call(bf16[512,512]{1,0:T(8,128)(2,1)S(1)} %bitcast.17, f32[512,512]{1,0:T(8,128)S(1)} %get-tuple-element.73.gates, bf16[512,512]{1,0:T(8,128)(2,1)S(1)} %get-tuple-element.44.refs_0_.refs_4_.masked, bf16[512,512]{1,0:T(8,128)(2,1)S(1)} %copy-done, bf16[512,512]{1,0:T(8,128)(2,1)S(1)} %get-tuple-element.74.back), custom_call_target="tpu_custom_call" | custom-call | flops 500000000 | bytes 4194304 | tf_op jit(solution)/shard_map/finish/pallas_call | solution.py:400
  (13 shorter events, 0.0 us)
Async XLA Ops:
  0.0 5.9 %copy-start.1 = (bf16[512,512]{1,0:T(8,128)(2,1)S(1)}, bf16[512,512]{1,0:T(8,128)(2,1)}, u32[]{:S(2)}) copy-start(bf16[512,512]{1,0:T(8,128)(2,1)} %refs_5_.1) | copy-start | bytes 1572868
  2.5 3.4 %copy-start.2 = (bf16[512,40]{0,1:T(8,128)(2,1)S(1)}, bf16[512,40]{0,1:T(8,128)(2,1)}, u32[]{:S(2)}) copy-start(bf16[512,40]{0,1:T(8,128)(2,1)} %param.18) | copy-start | bytes 122884
  2.5 3.3 %collective-permute-start = (bf16[144,512]{1,0:T(8,128)(2,1)S(1)}, bf16[144,512]{1,0:T(8,128)(2,1)S(1)}, u32[]{:S(2)}, u32[]{:S(2)}) collective-permute-start(bf16[144,512]{1,0:T(8,128)(2,1)S(1)} %get-tuple-element.41.own), channel_id=1, source_target_pairs={{0,1},{1,0},{2,3},{3,2},{4,5},{5,4},{6,7},{7,6},{8,9},{9,8},{10,11... | collective-permute-start | bytes 442376 | tf_op jit(solution)/shard_map/ppermute | solution.py:465
  5.9 0.7 copy-start.3
  7.8 7.0 %collective-permute-start.1 = (bf16[144,512]{1,0:T(8,128)(2,1)S(1)}, bf16[144,512]{1,0:T(8,128)(2,1)S(1)}, u32[]{:S(2)}, u32[]{:S(2)}) collective-permute-start(bf16[144,512]{1,0:T(8,128)(2,1)S(1)} %get-tuple-element.49.own), channel_id=1, source_target_pairs={{0,2},{1,3},{2,4},{3,5},{4,6},{5,7},{8,10},{9,11},{10,12},{11,13},... | collective-permute-start | bytes 442376 | tf_op jit(solution)/shard_map/ppermute | solution.py:380
  14.8 1.4 %copy-start.9 = (f32[8]{0:T(128)S(1)}, f32[8]{0:T(128)}, u32[]{:S(2)}) copy-start(f32[8]{0:T(128)} %param.27) | copy-start | bytes 100
  14.9 8.4 %collective-permute-start.2 = (bf16[128,512]{1,0:T(8,128)(2,1)S(1)}, bf16[128,512]{1,0:T(8,128)(2,1)S(1)}, u32[]{:S(2)}, u32[]{:S(2)}) collective-permute-start(bf16[128,512]{1,0:T(8,128)(2,1)S(1)} %get-tuple-element.58), channel_id=1, source_target_pairs={{0,4},{1,5},{2,6},{3,7},{8,12},{9,13},{10,14},{11,15},{16,20},{17,... | collective-permute-start | bytes 393224 | tf_op jit(solution)/shard_map/ppermute | solution.py:380
  16.2 0.7 copy-start.5
  16.2 0.7 copy-start.6
  16.2 0.7 copy-start.7
  16.2 0.7 copy-start.8
  24.2 28.4 %copy-start.4 = (bf16[512,40]{0,1:T(8,128)(2,1)S(1)}, bf16[512,40]{0,1:T(8,128)(2,1)}, u32[]{:S(2)}) copy-start(bf16[512,40]{0,1:T(8,128)(2,1)} %param.19) | copy-start | bytes 122884
  55.0 20.9 %copy-start = (bf16[512,512]{1,0:T(8,128)(2,1)S(1)}, bf16[512,512]{1,0:T(8,128)(2,1)}, u32[]{:S(2)}) copy-start(bf16[512,512]{1,0:T(8,128)(2,1)} %w_out.1) | copy-start | bytes 1572868

commit v7 on v5

--- a/solution.py
+++ b/solution.py
@@ -577,7 +577,7 @@
         outs=IN_PLACE,
         scratch=[
             pltpu.VMEM((count, width_all), bf16),
-            pltpu.SemaphoreType.DMA((2,)),
+            pltpu.SemaphoreType.DMA((4,)),
         ],
     )
     return mixed.reshape(patches.shape)

time: 77.9 us -> 78.1 us (level)
  no operation moved by 1% of the time
where the time goes in v7:
time: 78.1 us; the launch traced here: 77.7 us
  blocking collectives  49.2 us (63%)
  Pallas kernels  10.4 us (13%)
  waiting for transfers between devices  10.2 us (13%)
  starting transfers between devices  6.31 us (8%)
  local copies, waits for them, and re-layouts  1.35 us (2%)
    all_to_all x2, blocking collectives, on_device(): lax.all_to_all(x.reshape(split), 'rows', 0, 0, axis_index_groups=order(fi...  49.2 us
    pallas_call x9, Pallas kernels, call(): pl.pallas_call(body, out_shape=out_shape, in_specs=[ins] * len(args), out...  10.4 us
    ppermute x2, waiting for transfers between devices, shifted(): return lax.ppermute(value, axis, [(i, i + by) for i in range(count - by)])  8.88 us
    ppermute x2, starting transfers between devices, shifted(): return lax.ppermute(value, axis, [(i, i + by) for i in range(count - by)])  4.39 us
    ppermute x1, starting transfers between devices, on_device(): came = lax.ppermute(payload, 'cols', [(i, i ^ 1) for i in range(count_of)])  1.92 us
  transfers between devices with their start and end apart: 3, of which 3 were waited for; matrix products, arithmetic and copies ran while one was open for 0% of the time, Pallas kernels for 2%

profile of v7, /device:TPU:4, one launch (start us, length us, event | category | flops | bytes accessed | tf_op | source)
XLA Modules:
  0.0 77.7 jit_solution(3142248398553815463)
XLA Ops:
  0.0 2.5 %prepare.1 = (bf16[512,512]{1,0:T(8,128)(2,1)S(1)}, bf16[512,512]{1,0:T(8,128)(2,1)S(1)}, f32[16,512]{1,0:T(8,128)S(1)}, f32[32,128]{1,0:T(8,128)S(1)}, f32[32,1...) custom-call(bf16[512,512]{1,0:T(8,128)(2,1)} %bitcast.31, s32[8,64]{1,0:T(8,128)} %refs_1_.2, bf16[512,512]{1,0:T(8,128)(2,1)} %refs_2_.1, ...), custom_call_target="tpu_custom_call" | custom-call | flops 500000000 | bytes 4194304 | tf_op jit(solution)/shard_map/prepare/pallas_call | solution.py:399
  2.5 0.0 copy-start.2
  2.5 1.9 %collective-permute-start = (bf16[144,512]{1,0:T(8,128)(2,1)S(1)}, bf16[144,512]{1,0:T(8,128)(2,1)S(1)}, u32[]{:S(2)}, u32[]{:S(2)}) collective-permute-start(bf16[144,512]{1,0:T(8,128)(2,1)S(1)} %get-tuple-element.41.own), channel_id=1, source_target_pairs={{0,1},{1,0},{2,3},{3,2},{4,5},{5,4},{6,7},{7,6},{8,9},{9,8},{10,11... | collective-permute-start | bytes 442376 | tf_op jit(solution)/shard_map/ppermute | solution.py:464
  4.5 1.3 %collective-permute-done.came = bf16[144,512]{1,0:T(8,128)(2,1)S(1)} collective-permute-done((bf16[144,512]{1,0:T(8,128)(2,1)S(1)}, bf16[144,512]{1,0:T(8,128)(2,1)S(1)}, u32[]{:S(2)}, u32[]{:S(2)}) %collective-permute-start) | collective-permute-done | bytes 147488 | tf_op jit(solution)/shard_map/ppermute | solution.py:464
  5.8 0.1 first_step.1
  5.9 0.0 copy-start.3
  5.9 0.7 copy-done.3
  6.6 1.2 %gate_first.1 = (f32[512,512]{1,0:T(8,128)S(1)}, f32[512,40]{1,0:T(8,128)S(1)}, bf16[512,512]{1,0:T(8,128)(2,1)S(1)}, bf16[512,512]{1,0:T(8,128)(2,1)S(1)}) custom-call(bf16[512,512]{1,0:T(8,128)(2,1)S(1)} %get-tuple-element.44.refs_0_.refs_4_.masked, bf16[512,512]{1,0:T(8,128)(2,1)S(1)} %copy-done.1, bf16[40,512]{1,0:T(8,128)(2,1)S(1)} %bitcast.21, ...), custom_call_target="tpu_custom_call" | custom-call | flops 500000000 | bytes 4194304 | tf_op jit(solution)/shard_map/gate_first/pallas_call | solution.py:399
  7.8 3.1 %collective-permute-start.1 = (bf16[144,512]{1,0:T(8,128)(2,1)S(1)}, bf16[144,512]{1,0:T(8,128)(2,1)S(1)}, u32[]{:S(2)}, u32[]{:S(2)}) collective-permute-start(bf16[144,512]{1,0:T(8,128)(2,1)S(1)} %get-tuple-element.49.own), channel_id=1, source_target_pairs={{0,2},{1,3},{2,4},{3,5},{4,6},{5,7},{8,10},{9,11},{10,12},{11,13},... | collective-permute-start | bytes 442376 | tf_op jit(solution)/shard_map/ppermute | solution.py:379
  10.9 3.9 %collective-permute-done.1.came = bf16[144,512]{1,0:T(8,128)(2,1)S(1)} collective-permute-done((bf16[144,512]{1,0:T(8,128)(2,1)S(1)}, bf16[144,512]{1,0:T(8,128)(2,1)S(1)}, u32[]{:S(2)}, u32[]{:S(2)}) %collective-permute-start.1) | collective-permute-done | bytes 147488 | tf_op jit(solution)/shard_map/ppermute | solution.py:379
  14.8 0.1 second_step.1
  14.9 1.3 %collective-permute-start.2 = (bf16[128,512]{1,0:T(8,128)(2,1)S(1)}, bf16[128,512]{1,0:T(8,128)(2,1)S(1)}, u32[]{:S(2)}, u32[]{:S(2)}) collective-permute-start(bf16[128,512]{1,0:T(8,128)(2,1)S(1)} %get-tuple-element.58), channel_id=1, source_target_pairs={{0,4},{1,5},{2,6},{3,7},{8,12},{9,13},{10,14},{11,15},{16,20},{17,... | collective-permute-start | bytes 393224 | tf_op jit(solution)/shard_map/ppermute | solution.py:379
  16.2 0.0 copy-start.6
  16.2 0.0 copy-start.7
  16.3 0.6 copy-done.5
  16.9 0.0 copy-done.8
  16.9 1.4 %within_rows.1 = (f32[512,512]{1,0:T(8,128)S(1)}, f32[512,512]{1,0:T(8,128)S(1)}, f32[1,8]{1,0:T(1,128)S(1)}, f32[1,8]{1,0:T(1,128)S(1)}, f32[1,8]{1,0:T(1,128)S(1)}, /*index=5*/f32[1,512]{1,0:T(1,128)S(1)}) custom-call(bf16[512,512]{1,0:T(8,128)(2,1)S(1)} %get-tuple-element.59.values, f32[512,40]{1,0:T(8,128)S(1)} %get-tuple-element.60.proj, ...), custom_call_target="tpu_custom_call" | custom-call | flops 1000000000 | bytes 4194304 | tf_op jit(solution)/shard_map/within_rows/pallas_call | solution.py:399
  18.3 5.0 %collective-permute-done.2.came = bf16[128,512]{1,0:T(8,128)(2,1)S(1)} collective-permute-done((bf16[128,512]{1,0:T(8,128)(2,1)S(1)}, bf16[128,512]{1,0:T(8,128)(2,1)S(1)}, u32[]{:S(2)}, u32[]{:S(2)}) %collective-permute-start.2) | collective-permute-done | bytes 131104 | tf_op jit(solution)/shard_map/ppermute | solution.py:379
  23.3 1.0 %finish_rows.1 = bf16[512,512]{1,0:T(8,128)(2,1)S(1)} custom-call(f32[512,512]{1,0:T(8,128)S(1)} %get-tuple-element.64.outputs, f32[512,512]{1,0:T(8,128)S(1)} %get-tuple-element.65.reach, f32[512,40]{1,0:T(8,128)S(1)} %get-tuple-element.60.proj, f32[128,512]{1,0:T(8,128)S(1)} %get-tuple-element.66.states, f32[8,512]{1,0:T(8,128)S(1)} %get-tuple-element.67.spans, ...), custom_call_target="tpu_custom_call" | custom-call | flops 500000000 | bytes 4194304 | tf_op jit(solution)/shard_map/finish_rows/pallas_call | solution.py:399
  24.2 28.4 %all_to_all.10 = bf16[64,8,512]{2,1,0:T(8,128)(2,1)S(1)} all-to-all(bf16[64,8,512]{2,1,0:T(8,128)(2,1)S(1)} %bitcast.16), channel_id=1, replica_groups={{368,376,384,392,400,408,416,424,432,440,448,456,464,472,480,488,496,50..., dimensions={0} | all-to-all | bytes 1048576 | tf_op jit(solution)/shard_map/all_to_all | solution.py:551
  52.6 2.4 %scan_columns.1 = bf16[512,512]{1,0:T(8,128)(2,1)S(1)} custom-call(bf16[512,512]{1,0:T(8,128)(2,1)S(1)} %bitcast.18, bf16[40,512]{1,0:T(8,128)(2,1)S(1)} %bitcast.25, f32[1,8]{1,0:T(1,128)S(1)} %get-tuple-element.70.bias, f32[1,8]{1,0:T(1,128)S(1)} %get-tuple-element.71.rates, f32[1,8]{1,0:T(1,128)S(1)} %get-tuple-element.72.skips), custom_call_target="tpu_custom_call" | custom-call | flops 1000000000 | bytes 4194304 | tf_op jit(solution)/shard_map/scan_columns/pallas_call | solution.py:399
  55.0 0.0 copy-start
  55.0 20.9 %all_to_all.11 = bf16[64,8,512]{2,1,0:T(8,128)(2,1)S(1)} all-to-all(bf16[64,8,512]{2,1,0:T(8,128)(2,1)S(1)} %bitcast.19), channel_id=1, replica_groups={{368,376,384,392,400,408,416,424,432,440,448,456,464,472,480,488,496,50..., dimensions={0} | all-to-all | bytes 1048576 | tf_op jit(solution)/shard_map/all_to_all | solution.py:551
  75.9 1.8 %finish.1 = bf16[512,512]{1,0:T(8,128)(2,1)} custom-call(bf16[512,512]{1,0:T(8,128)(2,1)S(1)} %bitcast.17, f32[512,512]{1,0:T(8,128)S(1)} %get-tuple-element.73.gates, bf16[512,512]{1,0:T(8,128)(2,1)S(1)} %get-tuple-element.44.refs_0_.refs_4_.masked, bf16[512,512]{1,0:T(8,128)(2,1)S(1)} %copy-done, bf16[512,512]{1,0:T(8,128)(2,1)S(1)} %get-tuple-element.74.back), custom_call_target="tpu_custom_call" | custom-call | flops 500000000 | bytes 4194304 | tf_op jit(solution)/shard_map/finish/pallas_call | solution.py:399
  (13 shorter events, 0.0 us)
Async XLA Ops:
  0.0 5.9 %copy-start.1 = (bf16[512,512]{1,0:T(8,128)(2,1)S(1)}, bf16[512,512]{1,0:T(8,128)(2,1)}, u32[]{:S(2)}) copy-start(bf16[512,512]{1,0:T(8,128)(2,1)} %refs_5_.1) | copy-start | bytes 1572868
  2.5 3.4 %copy-start.2 = (bf16[512,40]{0,1:T(8,128)(2,1)S(1)}, bf16[512,40]{0,1:T(8,128)(2,1)}, u32[]{:S(2)}) copy-start(bf16[512,40]{0,1:T(8,128)(2,1)} %param.18) | copy-start | bytes 122884
  2.5 3.3 %collective-permute-start = (bf16[144,512]{1,0:T(8,128)(2,1)S(1)}, bf16[144,512]{1,0:T(8,128)(2,1)S(1)}, u32[]{:S(2)}, u32[]{:S(2)}) collective-permute-start(bf16[144,512]{1,0:T(8,128)(2,1)S(1)} %get-tuple-element.41.own), channel_id=1, source_target_pairs={{0,1},{1,0},{2,3},{3,2},{4,5},{5,4},{6,7},{7,6},{8,9},{9,8},{10,11... | collective-permute-start | bytes 442376 | tf_op jit(solution)/shard_map/ppermute | solution.py:464
  5.9 0.7 copy-start.3
  7.8 7.0 %collective-permute-start.1 = (bf16[144,512]{1,0:T(8,128)(2,1)S(1)}, bf16[144,512]{1,0:T(8,128)(2,1)S(1)}, u32[]{:S(2)}, u32[]{:S(2)}) collective-permute-start(bf16[144,512]{1,0:T(8,128)(2,1)S(1)} %get-tuple-element.49.own), channel_id=1, source_target_pairs={{0,2},{1,3},{2,4},{3,5},{4,6},{5,7},{8,10},{9,11},{10,12},{11,13},... | collective-permute-start | bytes 442376 | tf_op jit(solution)/shard_map/ppermute | solution.py:379
  14.8 1.4 %copy-start.9 = (f32[8]{0:T(128)S(1)}, f32[8]{0:T(128)}, u32[]{:S(2)}) copy-start(f32[8]{0:T(128)} %param.27) | copy-start | bytes 100
  14.9 8.4 %collective-permute-start.2 = (bf16[128,512]{1,0:T(8,128)(2,1)S(1)}, bf16[128,512]{1,0:T(8,128)(2,1)S(1)}, u32[]{:S(2)}, u32[]{:S(2)}) collective-permute-start(bf16[128,512]{1,0:T(8,128)(2,1)S(1)} %get-tuple-element.58), channel_id=1, source_target_pairs={{0,4},{1,5},{2,6},{3,7},{8,12},{9,13},{10,14},{11,15},{16,20},{17,... | collective-permute-start | bytes 393224 | tf_op jit(solution)/shard_map/ppermute | solution.py:379
  16.2 0.7 copy-start.5
  16.2 0.7 copy-start.6
  16.2 0.7 copy-start.7
  16.2 0.7 copy-start.8
  24.2 28.4 %copy-start.4 = (bf16[512,40]{0,1:T(8,128)(2,1)S(1)}, bf16[512,40]{0,1:T(8,128)(2,1)}, u32[]{:S(2)}) copy-start(bf16[512,40]{0,1:T(8,128)(2,1)} %param.19) | copy-start | bytes 122884
  55.0 20.9 %copy-start = (bf16[512,512]{1,0:T(8,128)(2,1)S(1)}, bf16[512,512]{1,0:T(8,128)(2,1)}, u32[]{:S(2)}) copy-start(bf16[512,512]{1,0:T(8,128)(2,1)} %w_out.1) | copy-start | bytes 1572868
